TPU v7x, 256 devices: a whole 4x4x8 slice. The times are simulated.
256 devices in a mesh: row: 8 (over y, x_lo), col: 32 (over x_hi, z, core).
Axes of the slice: x: 4 (x_hi: 2, x_lo: 2; x = x_hi * 2 + x_lo), y: 4, z: 8, core: 2. Of those that a mesh axis runs over, the one named last changes fastest.
Arguments:
- density: float32 [4096, 4096], P('row', 'col'), as said below
- pattern: int32 [32, 6], replicated, may hold values from 0 to 31, as said below
Outputs:
- purified: float32 [4096, 4096], P('row', 'col')
Inputs may be any that keep to these rules, and one draw needn't show every extreme that they name: density is symmetric. `pattern`: each row lists 6 different block columns; the first is the row's own index.
All inputs are finite; a program needn't handle non-finite values.
Results may differ from a plain program's by a relative error of at most 0.00021.
Values sent between devices are 32-bit elements; how exact they have to be, the bound alone decides.
No kernel may reach another device: no remote copies, remote signals or barrier semaphores. Data moves between devices by JAX's collectives and lax.ppermute only.
A program may use at most 64 MiB of HBM per device.

v0:
```python
import jax
import jax.numpy as jnp
from jax import lax
from jax.sharding import PartitionSpec as P

BLK = 128
NNZ = 6
ITERS = 2


def full_product(left, right):
    return jnp.dot(left, right, precision=lax.Precision.HIGHEST, preferred_element_type=jnp.float32)


def local(density, pattern):
    rows_dev, cols_dev = density.shape
    row_number = lax.axis_index("row")
    col_index = lax.axis_index("col")
    matrix_order = cols_dev * lax.axis_size("col")
    block_count = matrix_order // BLK
    tile_blocks = cols_dev // BLK
    row_blocks = rows_dev // BLK
    listed = jnp.any(
        pattern[:, :, None] == jnp.arange(block_count, dtype=jnp.int32)[None, None, :], axis=1
    ).astype(jnp.float32)
    block_live = jnp.maximum(listed, listed.T)
    my_rows = lax.dynamic_slice_in_dim(block_live, row_number * row_blocks, row_blocks, 0)
    own_blocks = lax.dynamic_slice_in_dim(my_rows, col_index * tile_blocks, tile_blocks, 1)
    pattern_mask = jnp.repeat(jnp.repeat(own_blocks, BLK, axis=0), BLK, axis=1)
    global_rows = row_number * rows_dev + jnp.arange(rows_dev, dtype=jnp.int32)
    global_cols = col_index * cols_dev + jnp.arange(cols_dev, dtype=jnp.int32)
    identity = (global_rows[:, None] == global_cols[None, :]).astype(jnp.float32)
    current = 0.5 * identity + 0.45 / jnp.sqrt(jnp.float32(2 * NNZ * BLK)) * pattern_mask * density
    for purify_round in range(ITERS):
        column_panel = lax.all_gather(current, "row", axis=0, tiled=True)
        row_panel = lax.all_gather(current, "col", axis=1, tiled=True)
        product = full_product(row_panel, column_panel)
        square = pattern_mask * product
        square_panel = lax.all_gather(square, "row", axis=0, tiled=True)
        cube = pattern_mask * full_product(row_panel, square_panel)
        current = 3.0 * square - 2.0 * cube
    return current


def solution(mesh):
    return jax.shard_map(
        local,
        mesh=mesh,
        in_specs=(P("row", "col"), P()),
        out_specs=P("row", "col"),
        check_vma=False,
    )
```

profile of v0, /device:TPU:1, one launch (start us, length us, event | category | flops | bytes accessed | tf_op | source)
XLA Modules:
  0.0 493.6 jit_solution(8498363634711816271)
XLA Ops:
  6.5 0.8 fusion.4
  7.4 0.1 dynamic_slice.8
  7.4 0.1 copy.6
  7.5 0.1 fusion.5
  7.6 0.1 bitcast_multiply_fusion
  7.7 1.9 multiply_add_fusion
  9.6 0.0 all-gather.7.cloned.1.call-start
  9.6 0.7 all-gather.7.cloned.1.call-update
  10.3 0.0 all-gather.11.cloned.1.call-start
  10.4 0.1 broadcast_bitcast_fusion
  10.4 57.6 %all-gather.9.cloned.1.call-done = f32[4096,128]{1,0:T(8,128)} async-done(((f32[512,128]{1,0:T(8,128)}), f32[4096,128]{1,0:T(8,128)}) %all-gather.9.cloned.1.call-update) | async-done | bytes 2097168 | tf_op jit(solution)/shard_map/all_gather | solution.py:35
  68.0 110.9 %all-gather.7.cloned.1.call-done = f32[512,4096]{1,0:T(8,128)} async-done(((f32[512,128]{1,0:T(8,128)}), f32[512,4096]{1,0:T(8,128)}) %all-gather.7.cloned.1.call-update) | async-done | bytes 8388624 | tf_op jit(solution)/shard_map/all_gather | solution.py:36
  178.9 10.4 %convolution_multiply_fusion.3 = f32[512,128]{1,0:T(8,128)} fusion(f32[512,4096]{1,0:T(8,128)} %all-gather.7.cloned.1.call-done, f32[4096,128]{1,0:T(8,128)} %all-gather.9.cloned.1.call-done, f32[512]{0:T(512)S(1)} %broadcast_bitcast_fusion), kind=kOutput, calls=%fused_computation.5 | convolution fusion | flops 3221291008 | bytes 10749952 | tf_op jit(solution)/shard_map/dot_general | solution.py:12
  189.3 0.0 all-gather.15.cloned.1.call-start
  189.4 50.5 %all-gather.11.cloned.1.call-done = f32[4096,128]{1,0:T(8,128)} async-done(((f32[512,128]{1,0:T(8,128)}), f32[4096,128]{1,0:T(8,128)}) %all-gather.11.cloned.1.call-update) | async-done | bytes 2097168 | tf_op jit(solution)/shard_map/all_gather | solution.py:39
  239.9 10.5 %fusion.2 = f32[512,128]{1,0:T(8,128)} fusion(f32[512,4096]{1,0:T(8,128)} %all-gather.7.cloned.1.call-done, f32[4096,128]{1,0:T(8,128)} %all-gather.11.cloned.1.call-done, f32[512,128]{1,0:T(8,128)} %convolution_multiply_fusion.3, f32[512]{0:T(512)S(1)} %broadcast_bitcast_fusion), kind=kOutput, calls=%fused_computation.6 | convolution fusion | flops 3221487616 | bytes 11012096 | tf_op jit(solution)/shard_map/dot_general | solution.py:12
  250.4 0.0 all-gather.13.cloned.1.call-start
  250.5 0.5 all-gather.13.cloned.1.call-update
  251.0 0.2 all-gather.17.cloned.1.call-start
  251.2 53.3 %all-gather.15.cloned.1.call-done = f32[4096,128]{1,0:T(8,128)} async-done(((f32[512,128]{1,0:T(8,128)}), f32[4096,128]{1,0:T(8,128)}) %all-gather.15.cloned.1.call-update) | async-done | bytes 2097168 | tf_op jit(solution)/shard_map/all_gather | solution.py:35
  304.5 110.7 %all-gather.13.cloned.1.call-done = f32[512,4096]{1,0:T(8,128)} async-done(((f32[512,128]{1,0:T(8,128)}), f32[512,4096]{1,0:T(8,128)}) %all-gather.13.cloned.1.call-update) | async-done | bytes 8388624 | tf_op jit(solution)/shard_map/all_gather | solution.py:36
  415.2 10.4 %convolution_multiply_fusion.1 = f32[512,128]{1,0:T(8,128)} fusion(f32[512,4096]{1,0:T(8,128)} %all-gather.13.cloned.1.call-done, f32[4096,128]{1,0:T(8,128)} %all-gather.15.cloned.1.call-done, f32[512]{0:T(512)S(1)} %broadcast_bitcast_fusion), kind=kOutput, calls=%fused_computation.2 | convolution fusion | flops 3221291008 | bytes 10749952 | tf_op jit(solution)/shard_map/dot_general | solution.py:12
  425.7 50.6 %all-gather.17.cloned.1.call-done = f32[4096,128]{1,0:T(8,128)} async-done(((f32[512,128]{1,0:T(8,128)}), f32[4096,128]{1,0:T(8,128)}) %all-gather.17.cloned.1.call-update) | async-done | bytes 2097168 | tf_op jit(solution)/shard_map/all_gather | solution.py:39
  476.3 10.5 %fusion.3 = f32[512,128]{1,0:T(8,128)} fusion(f32[512,4096]{1,0:T(8,128)} %all-gather.13.cloned.1.call-done, f32[4096,128]{1,0:T(8,128)} %all-gather.17.cloned.1.call-done, f32[512,128]{1,0:T(8,128)} %convolution_multiply_fusion.1, f32[512]{0:T(512)S(1)} %broadcast_bitcast_fusion), kind=kOutput, calls=%fused_computation.7 | convolution fusion | flops 3221487616 | bytes 11012096 | tf_op jit(solution)/shard_map/dot_general | solution.py:12
  (8 shorter events, 0.1 us)
Async XLA Ops:
  6.5 61.5 %all-gather.9.cloned.1.call-start = ((), (), s32[]{:S(2)}) async-start(), calls=%async_computation.1 | async-start | bytes 2359296 | tf_op jit(solution)/shard_map/all_gather | solution.py:35
  9.6 169.3 %all-gather.7.cloned.1.call-start = ((), (), s32[]{:S(2)}) async-start(), calls=%async_computation | async-start | bytes 8650752 | tf_op jit(solution)/shard_map/all_gather | solution.py:36
  10.3 229.6 %all-gather.11.cloned.1.call-start = ((), (), s32[]{:S(2)}) async-start(), calls=%async_computation.2 | async-start | bytes 2359296 | tf_op jit(solution)/shard_map/all_gather | solution.py:39
  189.3 115.2 %all-gather.15.cloned.1.call-start = ((), (), s32[]{:S(2)}) async-start(), calls=%async_computation.4 | async-start | bytes 2359296 | tf_op jit(solution)/shard_map/all_gather | solution.py:35
  250.4 164.8 %all-gather.13.cloned.1.call-start = ((), (), s32[]{:S(2)}) async-start(), calls=%async_computation.3 | async-start | bytes 8650752 | tf_op jit(solution)/shard_map/all_gather | solution.py:36
  251.0 225.3 %all-gather.17.cloned.1.call-start = ((), (), s32[]{:S(2)}) async-start(), calls=%async_computation.5 | async-start | bytes 2359296 | tf_op jit(solution)/shard_map/all_gather | solution.py:39
Sparse Core Ops, SparseCore 0:
  9.7 58.2 all-gather.8
  70.6 108.2 all-gather.6
  189.4 50.3 all-gather.10
  250.5 53.9 all-gather.14
  306.9 108.2 all-gather.12
  425.8 50.3 all-gather.16
where the time goes:
time: 494 us
  waiting for transfers between devices  435 us (88%)
  matrix products  41.9 us (8%)
  between operations  13.5 us (3%)
    all_gather x2, waiting for transfers between devices, local(): row_panel = lax.all_gather(current, 'col', axis=1, tiled=True)  222 us
    all_gather x2, waiting for transfers between devices, local(): column_panel = lax.all_gather(current, 'row', axis=0, tiled=True)  111 us
    all_gather x2, waiting for transfers between devices, local(): square_panel = lax.all_gather(square, 'row', axis=0, tiled=True)  101 us
    dot_general x4, matrix products, full_product(): jnp.dot(left, right, precision=lax.Precision.HIGHEST, preferred_element_t...  41.9 us
  transfers between devices with their start and end apart: 6, of which 6 were waited for; matrix products, arithmetic and copies ran while one was open for 0% of the time, Pallas kernels for 0%

commit v1 on v0

--- a/solution.py
+++ b/solution.py
@@ -8,8 +8,15 @@
 ITERS = 2
 
 
-def full_product(left, right):
-    return jnp.dot(left, right, precision=lax.Precision.HIGHEST, preferred_element_type=jnp.float32)
+def product(left, right):
+    return jnp.dot(left, right, precision=lax.Precision.HIGH, preferred_element_type=jnp.float32)
+
+
+def gather_rows(tile, name):
+    parts = lax.axis_size(name)
+    copies = jnp.broadcast_to(tile[None], (parts,) + tile.shape)
+    got = lax.all_to_all(copies, name, 0, 0)
+    return got.reshape(parts * tile.shape[0], tile.shape[1])
 
 
 def local(density, pattern):
@@ -32,12 +39,11 @@
     identity = (global_rows[:, None] == global_cols[None, :]).astype(jnp.float32)
     current = 0.5 * identity + 0.45 / jnp.sqrt(jnp.float32(2 * NNZ * BLK)) * pattern_mask * density
     for purify_round in range(ITERS):
-        column_panel = lax.all_gather(current, "row", axis=0, tiled=True)
         row_panel = lax.all_gather(current, "col", axis=1, tiled=True)
-        product = full_product(row_panel, column_panel)
-        square = pattern_mask * product
-        square_panel = lax.all_gather(square, "row", axis=0, tiled=True)
-        cube = pattern_mask * full_product(row_panel, square_panel)
+        column_panel = gather_rows(current, "row")
+        square = pattern_mask * product(row_panel, column_panel)
+        square_panel = gather_rows(square, "row")
+        cube = pattern_mask * product(row_panel, square_panel)
         current = 3.0 * square - 2.0 * cube
     return current
 

time: 494 us -> 323 us (0.65)
  waiting for transfers between devices: 435 us -> 182 us
  blocking collectives: 0 us -> 92.2 us
  matrix products: 41.9 us -> 21.7 us
  starting transfers between devices: 0.38 us -> 5.99 us
    all_gather x4 -> x0, waiting for transfers between devices: 212 us -> none  [the longest x2 111 us: local(): column_panel = lax.all_gather(current, 'row', axis=0, tiled=True)]
    all_to_all x0 -> x3, blocking collectives: none -> 92.2 us  [gather_rows(): got = lax.all_to_all(copies, name, 0, 0)]
    all_gather x2, waiting for transfers between devices: 222 us -> 154 us  [local(): row_panel = lax.all_gather(current, 'col', axis=1, tiled=True)]
    all_to_all x0 -> x1, waiting for transfers between devices: none -> 28.8 us  [gather_rows(): got = lax.all_to_all(copies, name, 0, 0)]
    dot_general x4, matrix products: 41.9 us -> 21.7 us  [product(): jnp.dot(left, right, precision=lax.Precision.HIGH, preferred_element_type...]
    all_to_all x0 -> x1, starting transfers between devices: none -> 5.95 us  [gather_rows(): got = lax.all_to_all(copies, name, 0, 0)]
  transfers between devices with their start and end apart: 6 -> 3, of which waited for: 6 -> 3; matrix products, arithmetic and copies ran while one was open for 0% -> 1% of each run, Pallas kernels for 0% -> 0%
where the time goes in v1:
time: 323 us
  waiting for transfers between devices  182 us (56%)
  blocking collectives  92.2 us (29%)
  matrix products  21.7 us (7%)
  between operations  13.5 us (4%)
  starting transfers between devices  5.99 us (2%)
  local copies, waits for them, and re-layouts  4.07 us (1%)
    all_gather x2, waiting for transfers between devices, local(): row_panel = lax.all_gather(current, 'col', axis=1, tiled=True)  154 us
    all_to_all x3, blocking collectives, gather_rows(): got = lax.all_to_all(copies, name, 0, 0)  92.2 us
    all_to_all x1, waiting for transfers between devices, gather_rows(): got = lax.all_to_all(copies, name, 0, 0)  28.8 us
    dot_general x4, matrix products, product(): jnp.dot(left, right, precision=lax.Precision.HIGH, preferred_element_type...  21.7 us
  transfers between devices with their start and end apart: 3, of which 3 were waited for; matrix products, arithmetic and copies ran while one was open for 1% of the time, Pallas kernels for 0%

profile of v1, /device:TPU:1, one launch (start us, length us, event | category | flops | bytes accessed | tf_op | source)
XLA Modules:
  0.0 322.7 jit_solution(1169803695684405316)
XLA Ops:
  6.5 0.8 fusion.4
  7.4 0.1 dynamic_slice.8
  7.4 0.1 copy.6
  7.5 0.1 fusion.5
  7.6 0.1 bitcast_multiply_fusion
  7.7 1.9 multiply_add_fusion
  9.5 0.0 all-gather.3.cloned.1.call-update
  9.6 2.5 broadcast_in_dim.14
  12.0 5.9 %all-to-all-start = ((f32[8,512,128]{2,1,0:T(8,128)}), f32[8,512,128]{2,1,0:T(8,128)S(1)}, u32[]{:S(2)}, u32[]{:S(2)}) async-start(f32[8,512,128]{2,1,0:T(8,128)} %broadcast_in_dim.14), calls=%async_computation | async-start | bytes 4194304 | tf_op jit(solution)/shard_map/all_to_all | solution.py:18
  18.0 0.0 all-gather.5.cloned.1.call-start
  18.0 0.1 broadcast_bitcast_fusion
  18.1 28.8 %all-to-all-done = f32[8,512,128]{2,1,0:T(8,128)S(1)} async-done(((f32[8,512,128]{2,1,0:T(8,128)}), f32[8,512,128]{2,1,0:T(8,128)S(1)}, u32[]{:S(2)}, u32[]{:S(2)}) %all-to-all-start) | async-done | bytes 2097184 | tf_op jit(solution)/shard_map/all_to_all | solution.py:18
  46.8 78.6 %all-gather.3.cloned.1.call-done = f32[512,4096]{1,0:T(8,128)} async-done(((f32[512,128]{1,0:T(8,128)}), f32[512,4096]{1,0:T(8,128)}) %all-gather.3.cloned.1.call-update) | async-done | bytes 8388624 | tf_op jit(solution)/shard_map/all_gather | solution.py:42
  125.5 6.7 %convolution_multiply_fusion.3 = f32[512,128]{1,0:T(8,128)S(1)} fusion(f32[512,4096]{1,0:T(8,128)} %all-gather.3.cloned.1.call-done, f32[4096,128]{1,0:T(8,128)S(1)} %bitcast.19, f32[512]{0:T(512)S(1)} %broadcast_bitcast_fusion), kind=kOutput, calls=%fused_computation.5 | convolution fusion | flops 1610678272 | bytes 10749952 | tf_op jit(solution)/shard_map/dot_general | solution.py:12
  132.2 0.1 broadcast_in_dim.15
  132.3 30.0 %all_to_all.20 = f32[8,512,128]{2,1,0:T(8,128)S(1)} all-to-all(f32[8,512,128]{2,1,0:T(8,128)S(1)} %broadcast_in_dim.15), channel_id=1, replica_groups=mesh['row'=8,'col'=32] {'row'}, dimensions={0} | all-to-all | bytes 4194304 | tf_op jit(solution)/shard_map/all_to_all | solution.py:18
  162.4 4.2 %fusion.2 = f32[512,128]{1,0:T(8,128)} fusion(f32[512,4096]{1,0:T(8,128)S(1)} %copy-done, f32[4096,128]{1,0:T(8,128)S(1)} %bitcast.22, f32[512,128]{1,0:T(8,128)S(1)} %convolution_multiply_fusion.3, f32[512]{0:T(512)S(1)} %broadcast_bitcast_fusion), kind=kOutput, calls=%fused_computation.6 | convolution fusion | flops 1610874880 | bytes 11012096 | tf_op jit(solution)/shard_map/dot_general | solution.py:12
  166.6 1.1 broadcast_in_dim.16
  167.7 32.1 %all_to_all.21 = f32[8,512,128]{2,1,0:T(8,128)S(1)} all-to-all(f32[8,512,128]{2,1,0:T(8,128)S(1)} %broadcast_in_dim.16), channel_id=1, replica_groups=mesh['row'=8,'col'=32] {'row'}, dimensions={0} | all-to-all | bytes 4194304 | tf_op jit(solution)/shard_map/all_to_all | solution.py:18
  199.8 75.0 %all-gather.5.cloned.1.call-done = f32[512,4096]{1,0:T(8,128)} async-done(((f32[512,128]{1,0:T(8,128)}), f32[512,4096]{1,0:T(8,128)}) %all-gather.5.cloned.1.call-update) | async-done | bytes 8388624 | tf_op jit(solution)/shard_map/all_gather | solution.py:42
  274.8 6.7 %convolution_multiply_fusion.1 = f32[512,128]{1,0:T(8,128)S(1)} fusion(f32[512,4096]{1,0:T(8,128)} %all-gather.5.cloned.1.call-done, f32[4096,128]{1,0:T(8,128)S(1)} %bitcast.20, f32[512]{0:T(512)S(1)} %broadcast_bitcast_fusion), kind=kOutput, calls=%fused_computation.2 | convolution fusion | flops 1610678272 | bytes 10749952 | tf_op jit(solution)/shard_map/dot_general | solution.py:12
  281.5 0.1 broadcast_in_dim.17
  281.7 30.0 %all_to_all.22 = f32[8,512,128]{2,1,0:T(8,128)S(1)} all-to-all(f32[8,512,128]{2,1,0:T(8,128)S(1)} %broadcast_in_dim.17), channel_id=1, replica_groups=mesh['row'=8,'col'=32] {'row'}, dimensions={0} | all-to-all | bytes 4194304 | tf_op jit(solution)/shard_map/all_to_all | solution.py:18
  311.7 4.2 %fusion.3 = f32[512,128]{1,0:T(8,128)} fusion(f32[512,4096]{1,0:T(8,128)S(1)} %copy-done.1, f32[4096,128]{1,0:T(8,128)S(1)} %bitcast.21, f32[512,128]{1,0:T(8,128)S(1)} %convolution_multiply_fusion.1, f32[512]{0:T(512)S(1)} %broadcast_bitcast_fusion), kind=kOutput, calls=%fused_computation.7 | convolution fusion | flops 1610874880 | bytes 11012096 | tf_op jit(solution)/shard_map/dot_general | solution.py:12
  (9 shorter events, 0.0 us)
Async XLA Ops:
  6.5 118.9 %all-gather.3.cloned.1.call-start = ((), (), s32[]{:S(2)}) async-start(), calls=%async_computation.4 | async-start | bytes 8650752 | tf_op jit(solution)/shard_map/all_gather | solution.py:42
  12.0 34.8 %all-to-all-start = ((f32[8,512,128]{2,1,0:T(8,128)}), f32[8,512,128]{2,1,0:T(8,128)S(1)}, u32[]{:S(2)}, u32[]{:S(2)}) async-start(f32[8,512,128]{2,1,0:T(8,128)} %broadcast_in_dim.14), calls=%async_computation | async-start | bytes 4194304 | tf_op jit(solution)/shard_map/all_to_all | solution.py:18
  18.0 256.8 %all-gather.5.cloned.1.call-start = ((), (), s32[]{:S(2)}) async-start(), calls=%async_computation.5 | async-start | bytes 8650752 | tf_op jit(solution)/shard_map/all_gather | solution.py:42
  125.5 36.9 %copy-start = (f32[512,4096]{1,0:T(8,128)S(1)}, f32[512,4096]{1,0:T(8,128)}, u32[]{:S(2)}) copy-start(f32[512,4096]{1,0:T(8,128)} %all-gather.3.cloned.1.call-done) | copy-start | bytes 25165828
  274.8 36.9 %copy-start.1 = (f32[512,4096]{1,0:T(8,128)S(1)}, f32[512,4096]{1,0:T(8,128)}, u32[]{:S(2)}) copy-start(f32[512,4096]{1,0:T(8,128)} %all-gather.5.cloned.1.call-done) | copy-start | bytes 25165828
Sparse Core Ops, SparseCore 0:
  9.9 115.5 all-gather.2
  166.7 108.0 all-gather.4

commit v2 on v1

v2 whole, which is shorter than its diff:
```python
import jax
import jax.numpy as jnp
from jax import lax
from jax.experimental import pallas as pl
from jax.experimental.pallas import tpu as pltpu
from jax.sharding import PartitionSpec as P

BLK = 128
NNZ = 6
ITERS = 2
X_HI, Z, CORE = 2, 8, 2
GROUP = 4


def gather_rows(tile, name):
    parts = lax.axis_size(name)
    copies = jnp.broadcast_to(tile[None], (parts,) + tile.shape)
    got = lax.all_to_all(copies, name, 0, 0)
    return got.reshape(parts * tile.shape[0], tile.shape[1])


def col_id(x_hi, z, core):
    return (x_hi * Z + z % Z) * CORE + core


COLS = [(x, z, c) for x in range(X_HI) for z in range(Z) for c in range(CORE)]
UP = [(col_id(x, z, c), col_id(x, z + 1, c)) for x, z, c in COLS]
DOWN = [(col_id(x, z, c), col_id(x, z - 1, c)) for x, z, c in COLS]
ACROSS = [(col_id(x, z, c), col_id(1 - x, z, c)) for x, z, c in COLS]
TWIN = [(col_id(x, z, c), col_id(x, z, 1 - c)) for x, z, c in COLS]


def gather_cols(tile):
    send = lambda v, pairs: lax.ppermute(v, "col", pairs)
    both = jnp.stack([tile, send(tile, ACROSS)])
    up = down = both
    pieces = [both]
    for _ in range(3):
        up, down = send(up, UP), send(down, DOWN)
        pieces += [up, down]
    pieces += [send(up[:1], UP), send(down[1:], DOWN)]
    return pieces + [send(p, TWIN) for p in pieces]


def piece_columns(col):
    x_hi, z, core = col // (Z * CORE), (col // CORE) % Z, col % CORE
    out = []
    for c in (core, 1 - core):
        for d in (0, -1, 1, -2, 2, -3, 3):
            out += [col_id(x_hi, z + d + Z, c), col_id(1 - x_hi, z + d + Z, c)]
        out += [col_id(x_hi, z + 4, c), col_id(1 - x_hi, z + 4, c)]
    return jnp.stack(out).astype(jnp.int32)


def split(x):
    high = x.astype(jnp.bfloat16)
    return high, (x - high.astype(jnp.float32)).astype(jnp.bfloat16)


def product_body(sizes, combine, columns, live, *refs):
    pieces = refs[: len(sizes)]
    panel = refs[len(sizes)]
    square = refs[len(sizes) + 1] if combine else None
    out, held, total, sems = refs[-4:]
    slot = 0
    for piece, n in zip(pieces, sizes):
        for j in range(n):
            pltpu.make_async_copy(piece.at[j], held.at[slot], sems.at[slot]).start()
            slot += 1
    total[...] = jnp.zeros_like(total)

    def step(g, carry):
        left, right = [], []
        for q in range(GROUP):
            s = g * GROUP + q
            pltpu.make_async_copy(held.at[s], held.at[s], sems.at[s]).wait()
            left.append(held[s])
            right.append(panel[pl.ds(pl.multiple_of(columns[s] * BLK, BLK), BLK), :])
        left_high, left_low = split(jnp.concatenate(left, axis=1))
        right_high, right_low = split(jnp.concatenate(right, axis=0))
        wide = jnp.dot(
            left_high,
            jnp.concatenate([right_high, right_low], axis=1),
            preferred_element_type=jnp.float32,
        )
        narrow = jnp.dot(left_low, right_high, preferred_element_type=jnp.float32)
        total[...] += (wide[:, BLK:] + narrow) + wide[:, :BLK]
        return carry

    lax.fori_loop(0, held.shape[0] // GROUP, step, 0)
    for i in range(out.shape[0] // BLK):
        rows = pl.ds(i * BLK, BLK)
        masked = live[i] * total[rows, :]
        out[rows, :] = 3.0 * square[rows, :] - 2.0 * masked if combine else masked


def product(columns, live, pieces, panel, square=None):
    rows = pieces[0].shape[1]
    sizes = [p.shape[0] for p in pieces]
    slots = sum(sizes)
    smem = pl.BlockSpec(memory_space=pltpu.SMEM)
    vmem = pl.BlockSpec(memory_space=pltpu.VMEM)
    combine = square is not None
    body = lambda *refs: product_body(sizes, combine, *refs)
    return pl.pallas_call(
        body,
        out_shape=jax.ShapeDtypeStruct((rows, BLK), jnp.float32),
        in_specs=[smem, smem]
        + [pl.BlockSpec(memory_space=pl.ANY)] * len(pieces)
        + [vmem] * (2 if combine else 1),
        out_specs=vmem,
        scratch_shapes=[
            pltpu.VMEM((slots, rows, BLK), jnp.float32),
            pltpu.VMEM((rows, BLK), jnp.float32),
            pltpu.SemaphoreType.DMA((slots,)),
        ],
        compiler_params=pltpu.CompilerParams(vmem_limit_bytes=32 << 20),
        cost_estimate=pl.CostEstimate(
            flops=6 * rows * slots * BLK * BLK,
            bytes_accessed=4 * BLK * (slots * (rows + BLK) + 2 * rows),
            transcendentals=0,
        ),
    )(columns, live, *pieces, panel, *([square] if combine else []))


def local(density, pattern):
    rows_dev, cols_dev = density.shape
    row_number = lax.axis_index("row")
    col_index = lax.axis_index("col")
    matrix_order = cols_dev * lax.axis_size("col")
    block_count = matrix_order // BLK
    row_blocks = rows_dev // BLK
    listed = jnp.any(
        pattern[:, :, None] == jnp.arange(block_count, dtype=jnp.int32)[None, None, :], axis=1
    ).astype(jnp.float32)
    block_live = jnp.maximum(listed, listed.T)
    my_rows = lax.dynamic_slice_in_dim(block_live, row_number * row_blocks, row_blocks, 0)
    live = lax.dynamic_slice_in_dim(my_rows, col_index, 1, 1)[:, 0]
    pattern_mask = jnp.repeat(live, BLK)[:, None]
    global_rows = row_number * rows_dev + jnp.arange(rows_dev, dtype=jnp.int32)
    global_cols = col_index * cols_dev + jnp.arange(cols_dev, dtype=jnp.int32)
    identity = (global_rows[:, None] == global_cols[None, :]).astype(jnp.float32)
    current = 0.5 * identity + 0.45 / jnp.sqrt(jnp.float32(2 * NNZ * BLK)) * pattern_mask * density
    columns = piece_columns(col_index)
    for purify_round in range(ITERS):
        column_panel = lax.all_gather(current, "row", axis=0, tiled=True)
        pieces = gather_cols(current)
        square = product(columns, live, pieces, column_panel)
        square_panel = gather_rows(square, "row")
        current = product(columns, live, pieces, square_panel, square)
    return current


def solution(mesh):
    return jax.shard_map(
        local,
        mesh=mesh,
        in_specs=(P("row", "col"), P()),
        out_specs=P("row", "col"),
        check_vma=False,
    )
```

time: 323 us -> 256 us (0.79)
  waiting for transfers between devices: 182 us -> 58.8 us
  starting transfers between devices: 5.99 us -> 61.1 us
  blocking collectives: 92.2 us -> 62.8 us
  local copies, waits for them, and re-layouts: 4.07 us -> 30.1 us
  Pallas kernels: 0 us -> 23.7 us
  matrix products: 21.7 us -> 0 us
    all_gather x2, waiting for transfers between devices: 154 us -> 0.01 us  [local(): column_panel = lax.all_gather(current, 'row', axis=0, tiled=True)]
    ppermute x0 -> x36, starting transfers between devices: none -> 61.1 us  [gather_cols(): send = lambda v, pairs: lax.ppermute(v, 'col', pairs)]
    ppermute x0 -> x36, waiting for transfers between devices: none -> 58.7 us  [gather_cols(): send = lambda v, pairs: lax.ppermute(v, 'col', pairs)]
    unnamed x5 -> x65, local copies, waits for them, and re-layouts: 0.1 us -> 29.5 us
    all_to_all x3 -> x2, blocking collectives: 92.2 us -> 62.8 us  [gather_rows(): got = lax.all_to_all(copies, name, 0, 0)]
    all_to_all x1 -> x0, waiting for transfers between devices: 28.8 us -> none  [gather_rows(): got = lax.all_to_all(copies, name, 0, 0)]
    pallas_call x0 -> x4, Pallas kernels: none -> 23.7 us  [product(): pl.pallas_call(body, out_shape=jax.ShapeDtypeStruct((rows, BLK), jnp.floa...]
    dot_general x4 -> x0, matrix products: 21.7 us -> none  [product(): jnp.dot(left, right, precision=lax.Precision.HIGH, preferred_element_type...]
  transfers between devices with their start and end apart: 3 -> 38, of which waited for: 3 -> 13; matrix products, arithmetic and copies ran while one was open for 1% -> 1% of each run, Pallas kernels for 0% -> 0%
where the time goes in v2:
time: 256 us; the launch traced here: 255 us
  blocking collectives  62.8 us (25%)
  starting transfers between devices  61.1 us (24%)
  waiting for transfers between devices  58.8 us (23%)
  local copies, waits for them, and re-layouts  30.1 us (12%)
  Pallas kernels  23.7 us (9%)
  between operations  13.7 us (5%)
  other arithmetic  4.89 us (2%)
    all_to_all x2, blocking collectives, gather_rows(): got = lax.all_to_all(copies, name, 0, 0)  62.8 us
    ppermute x36, starting transfers between devices, gather_cols(): send = lambda v, pairs: lax.ppermute(v, 'col', pairs)  61.1 us
    ppermute x36, waiting for transfers between devices, gather_cols(): send = lambda v, pairs: lax.ppermute(v, 'col', pairs)  58.7 us
    unnamed x65, local copies, waits for them, and re-layouts  29.5 us
    pallas_call x4, Pallas kernels, product(): pl.pallas_call(body, out_shape=jax.ShapeDtypeStruct((rows, BLK), jnp.floa...  23.7 us
  transfers between devices with their start and end apart: 38, of which 13 were waited for; matrix products, arithmetic and copies ran while one was open for 1% of the time, Pallas kernels for 0%

profile of v2, /device:TPU:1, one launch (start us, length us, event | category | flops | bytes accessed | tf_op | source)
XLA Modules:
  0.0 255.1 jit_solution(11737176303885185787)
XLA Ops:
  9.6 3.7 %collective-permute-start = (f32[512,128]{1,0:T(8,128)}, f32[512,128]{1,0:T(8,128)S(1)}, u32[]{:S(2)}, u32[]{:S(2)}) collective-permute-start(f32[512,128]{1,0:T(8,128)} %multiply_add_fusion), channel_id=1, source_target_pairs={{0,16},{1,17},{2,18},{3,19},{4,20},{5,21},{6,22},{7,23},{8,24},{9,... | collective-permute-start | bytes 786440 | tf_op jit(solution)/shard_map/ppermute | solution.py:34
  14.4 4.1 %collective-permute-done = f32[512,128]{1,0:T(8,128)S(1)} collective-permute-done((f32[512,128]{1,0:T(8,128)}, f32[512,128]{1,0:T(8,128)S(1)}, u32[]{:S(2)}, u32[]{:S(2)}) %collective-permute-start) | collective-permute-done | bytes 262176 | tf_op jit(solution)/shard_map/ppermute | solution.py:34
  18.6 6.5 %collective-permute-start.2 = (f32[2,512,128]{2,1,0:T(8,128)S(1)}, f32[2,512,128]{2,1,0:T(8,128)S(1)}, u32[]{:S(2)}, u32[]{:S(2)}) collective-permute-start(f32[2,512,128]{2,1,0:T(8,128)S(1)} %pad_maximum_fusion.refs_2_), channel_id=1, source_target_pairs={{0,14},{1,15},{2,0},{3,1},{4,2},{5,3},{6,4},{7,5},{8,6},{9,7},{10,... | collective-permute-start | bytes 1572872 | tf_op jit(solution)/shard_map/ppermute | solution.py:34
  25.1 9.7 %collective-permute-done.2.refs_4_ = f32[2,512,128]{2,1,0:T(8,128)S(1)} collective-permute-done((f32[2,512,128]{2,1,0:T(8,128)S(1)}, f32[2,512,128]{2,1,0:T(8,128)S(1)}, u32[]{:S(2)}, u32[]{:S(2)}) %collective-permute-start.2) | collective-permute-done | bytes 524320 | tf_op jit(solution)/shard_map/ppermute | solution.py:34
  34.8 3.5 %collective-permute-start.4 = (f32[2,512,128]{2,1,0:T(8,128)S(1)}, f32[2,512,128]{2,1,0:T(8,128)S(1)}, u32[]{:S(2)}, u32[]{:S(2)}) collective-permute-start(f32[2,512,128]{2,1,0:T(8,128)S(1)} %collective-permute-done.2.refs_4_), channel_id=1, source_target_pairs={{0,14},{1,15},{2,0},{3,1},{4,2},{5,3},{6,4},{7,5},{8,6},{9,7},{10,... | collective-permute-start | bytes 1572872 | tf_op jit(solution)/shard_map/ppermute | solution.py:34
  38.3 8.8 %collective-permute-done.4.refs_6_ = f32[2,512,128]{2,1,0:T(8,128)S(1)} collective-permute-done((f32[2,512,128]{2,1,0:T(8,128)S(1)}, f32[2,512,128]{2,1,0:T(8,128)S(1)}, u32[]{:S(2)}, u32[]{:S(2)}) %collective-permute-start.4) | collective-permute-done | bytes 524320 | tf_op jit(solution)/shard_map/ppermute | solution.py:34
  47.1 3.4 %collective-permute-start.6 = (f32[2,512,128]{2,1,0:T(8,128)S(1)}, f32[2,512,128]{2,1,0:T(8,128)S(1)}, u32[]{:S(2)}, u32[]{:S(2)}) collective-permute-start(f32[2,512,128]{2,1,0:T(8,128)S(1)} %collective-permute-done.4.refs_6_), channel_id=1, source_target_pairs={{0,14},{1,15},{2,0},{3,1},{4,2},{5,3},{6,4},{7,5},{8,6},{9,7},{10,... | collective-permute-start | bytes 1572872 | tf_op jit(solution)/shard_map/ppermute | solution.py:34
  50.6 3.6 %collective-permute-start.9 = (f32[2,512,128]{2,1,0:T(8,128)S(1)}, f32[2,512,128]{2,1,0:T(8,128)S(1)}, u32[]{:S(2)}, u32[]{:S(2)}) collective-permute-start(f32[2,512,128]{2,1,0:T(8,128)S(1)} %pad_maximum_fusion.refs_2_), channel_id=1, source_target_pairs={{0,1},{1,0},{2,3},{3,2},{4,5},{5,4},{6,7},{7,6},{8,9},{9,8},{10,11... | collective-permute-start | bytes 1572872 | tf_op jit(solution)/shard_map/ppermute | solution.py:34
  54.6 3.8 %collective-permute-done.6.refs_8_ = f32[2,512,128]{2,1,0:T(8,128)S(1)} collective-permute-done((f32[2,512,128]{2,1,0:T(8,128)S(1)}, f32[2,512,128]{2,1,0:T(8,128)S(1)}, u32[]{:S(2)}, u32[]{:S(2)}) %collective-permute-start.6) | collective-permute-done | bytes 524320 | tf_op jit(solution)/shard_map/ppermute | solution.py:34
  58.5 4.2 %collective-permute-start.13 = (f32[2,512,128]{2,1,0:T(8,128)S(1)}, f32[2,512,128]{2,1,0:T(8,128)S(1)}, u32[]{:S(2)}, u32[]{:S(2)}) collective-permute-start(f32[2,512,128]{2,1,0:T(8,128)S(1)} %collective-permute-done.4.refs_6_), channel_id=1, source_target_pairs={{0,1},{1,0},{2,3},{3,2},{4,5},{5,4},{6,7},{7,6},{8,9},{9,8},{10,11... | collective-permute-start | bytes 1572872 | tf_op jit(solution)/shard_map/ppermute | solution.py:34
  62.7 3.6 %collective-permute-start.12 = (f32[2,512,128]{2,1,0:T(8,128)}, f32[2,512,128]{2,1,0:T(8,128)}, u32[]{:S(2)}, u32[]{:S(2)}) collective-permute-start(f32[2,512,128]{2,1,0:T(8,128)} %collective-permute-done.3.refs_5_), channel_id=1, source_target_pairs={{0,1},{1,0},{2,3},{3,2},{4,5},{5,4},{6,7},{7,6},{8,9},{9,8},{10,11... | collective-permute-start | bytes 1572872 | tf_op jit(solution)/shard_map/ppermute | solution.py:34
  71.6 3.6 %collective-permute-done.8.refs_10_ = f32[1,512,128]{2,1,0:T(8,128)S(1)} collective-permute-done((f32[1,512,128]{2,1,0:T(8,128)S(1)}, f32[1,512,128]{2,1,0:T(8,128)S(1)}, u32[]{:S(2)}, u32[]{:S(2)}) %collective-permute-start.8) | collective-permute-done | bytes 262176 | tf_op jit(solution)/shard_map/ppermute | solution.py:34
  85.3 5.5 %shard_map.28.refs_21_ = f32[512,128]{1,0:T(8,128)S(1)} custom-call(s32[32]{0:T(128)S(1)} %stack.149.refs_0_, f32[4]{0:T(128)S(1)} %get-tuple-element.6.refs_1_, f32[2,512,128]{2,1,0:T(8,128)S(1)} %pad_maximum_fusion.refs_2_, f32[2,512,128]{2,1,0:T(8,128)S(1)} %collective-permute-done.1.refs_3_, f32[2,512,128]{2,1,0:T(8,128)S(1)} %collective-permute-done.2.refs_4_, ...), custom_call_target="tpu_custom_call" | custom-call | flops 1610612736 | bytes 11010048 | tf_op jit(solution)/shard_map/pallas_call | solution.py:105
  91.0 31.1 %all_to_all.10 = f32[8,512,128]{2,1,0:T(8,128)S(1)} all-to-all(f32[8,512,128]{2,1,0:T(8,128)S(1)} %broadcast_in_dim.7), channel_id=1, replica_groups=mesh['row'=8,'col'=32] {'row'}, dimensions={0} | all-to-all | bytes 4194304 | tf_op jit(solution)/shard_map/all_to_all | solution.py:18
  122.1 6.3 %shard_map.29 = f32[512,128]{1,0:T(8,128)} custom-call(s32[32]{0:T(128)S(1)} %stack.149.refs_0_, f32[4]{0:T(128)S(1)} %get-tuple-element.6.refs_1_, f32[2,512,128]{2,1,0:T(8,128)S(1)} %pad_maximum_fusion.refs_2_, f32[2,512,128]{2,1,0:T(8,128)S(1)} %collective-permute-done.1.refs_3_, f32[2,512,128]{2,1,0:T(8,128)S(1)} %collective-permute-done.2.refs_4_, ...), custom_call_target="tpu_custom_call" | custom-call | flops 1610612736 | bytes 11010048 | tf_op jit(solution)/shard_map/pallas_call | solution.py:105
  130.9 5.1 %collective-permute-done.18 = f32[512,128]{1,0:T(8,128)S(1)} collective-permute-done((f32[512,128]{1,0:T(8,128)}, f32[512,128]{1,0:T(8,128)S(1)}, u32[]{:S(2)}, u32[]{:S(2)}) %collective-permute-start.18) | collective-permute-done | bytes 262176 | tf_op jit(solution)/shard_map/ppermute | solution.py:34
  138.6 8.1 %collective-permute-done.20.refs_4_ = f32[2,512,128]{2,1,0:T(8,128)S(1)} collective-permute-done((f32[2,512,128]{2,1,0:T(8,128)S(1)}, f32[2,512,128]{2,1,0:T(8,128)S(1)}, u32[]{:S(2)}, u32[]{:S(2)}) %collective-permute-start.20) | collective-permute-done | bytes 524320 | tf_op jit(solution)/shard_map/ppermute | solution.py:34
  148.2 9.0 %collective-permute-done.22.refs_6_ = f32[2,512,128]{2,1,0:T(8,128)S(1)} collective-permute-done((f32[2,512,128]{2,1,0:T(8,128)S(1)}, f32[2,512,128]{2,1,0:T(8,128)S(1)}, u32[]{:S(2)}, u32[]{:S(2)}) %collective-permute-start.22) | collective-permute-done | bytes 524320 | tf_op jit(solution)/shard_map/ppermute | solution.py:34
  158.7 8.4 %collective-permute-start.27 = (f32[2,512,128]{2,1,0:T(8,128)S(1)}, f32[2,512,128]{2,1,0:T(8,128)S(1)}, u32[]{:S(2)}, u32[]{:S(2)}) collective-permute-start(f32[2,512,128]{2,1,0:T(8,128)S(1)} %pad_maximum_fusion.1.refs_2_), channel_id=1, source_target_pairs={{0,1},{1,0},{2,3},{3,2},{4,5},{5,4},{6,7},{7,6},{8,9},{9,8},{10,11... | collective-permute-start | bytes 1572872 | tf_op jit(solution)/shard_map/ppermute | solution.py:34
  168.1 6.2 %collective-permute-start.31 = (f32[2,512,128]{2,1,0:T(8,128)S(1)}, f32[2,512,128]{2,1,0:T(8,128)S(1)}, u32[]{:S(2)}, u32[]{:S(2)}) collective-permute-start(f32[2,512,128]{2,1,0:T(8,128)S(1)} %collective-permute-done.22.refs_6_), channel_id=1, source_target_pairs={{0,1},{1,0},{2,3},{3,2},{4,5},{5,4},{6,7},{7,6},{8,9},{9,8},{10,11... | collective-permute-start | bytes 1572872 | tf_op jit(solution)/shard_map/ppermute | solution.py:34
  180.9 3.5 %collective-permute-done.26.refs_10_ = f32[1,512,128]{2,1,0:T(8,128)S(1)} collective-permute-done((f32[1,512,128]{2,1,0:T(8,128)S(1)}, f32[1,512,128]{2,1,0:T(8,128)S(1)}, u32[]{:S(2)}, u32[]{:S(2)}) %collective-permute-start.26) | collective-permute-done | bytes 262176 | tf_op jit(solution)/shard_map/ppermute | solution.py:34
  204.4 5.6 %shard_map.30.refs_21_ = f32[512,128]{1,0:T(8,128)S(1)} custom-call(s32[32]{0:T(128)S(1)} %stack.149.refs_0_, f32[4]{0:T(128)S(1)} %get-tuple-element.6.refs_1_, f32[2,512,128]{2,1,0:T(8,128)S(1)} %pad_maximum_fusion.1.refs_2_, f32[2,512,128]{2,1,0:T(8,128)S(1)} %collective-permute-done.19.refs_3_, f32[2,512,128]{2,1,0:T(8,128)S(1)} %collective-permute-done.20.refs_4_, ...), custom_call_target="tpu_custom_call" | custom-call | flops 1610612736 | bytes 11010048 | tf_op jit(solution)/shard_map/pallas_call | solution.py:105
  210.2 31.7 %all_to_all.11 = f32[8,512,128]{2,1,0:T(8,128)S(1)} all-to-all(f32[8,512,128]{2,1,0:T(8,128)S(1)} %broadcast_in_dim.8), channel_id=1, replica_groups=mesh['row'=8,'col'=32] {'row'}, dimensions={0} | all-to-all | bytes 4194304 | tf_op jit(solution)/shard_map/all_to_all | solution.py:18
  241.9 6.3 %shard_map.31 = f32[512,128]{1,0:T(8,128)} custom-call(s32[32]{0:T(128)S(1)} %stack.149.refs_0_, f32[4]{0:T(128)S(1)} %get-tuple-element.6.refs_1_, f32[2,512,128]{2,1,0:T(8,128)S(1)} %pad_maximum_fusion.1.refs_2_, f32[2,512,128]{2,1,0:T(8,128)S(1)} %collective-permute-done.19.refs_3_, f32[2,512,128]{2,1,0:T(8,128)S(1)} %collective-permute-done.20.refs_4_, ...), custom_call_target="tpu_custom_call" | custom-call | flops 1610612736 | bytes 11010048 | tf_op jit(solution)/shard_map/pallas_call | solution.py:105
  (143 shorter events, 56.0 us)
Async XLA Ops:
  6.5 73.0 %all-gather.3.cloned.1.call-start = ((), (), s32[]{:S(2)}) async-start(), calls=%async_computation.2 | async-start | bytes 2359296 | tf_op jit(solution)/shard_map/all_gather | solution.py:146
  9.6 182.1 %all-gather.5.cloned.1.call-start = ((), (), s32[]{:S(2)}) async-start(), calls=%async_computation.3 | async-start | bytes 2359296 | tf_op jit(solution)/shard_map/all_gather | solution.py:146
  18.6 16.2 %collective-permute-start.2 = (f32[2,512,128]{2,1,0:T(8,128)S(1)}, f32[2,512,128]{2,1,0:T(8,128)S(1)}, u32[]{:S(2)}, u32[]{:S(2)}) collective-permute-start(f32[2,512,128]{2,1,0:T(8,128)S(1)} %pad_maximum_fusion.refs_2_), channel_id=1, source_target_pairs={{0,14},{1,15},{2,0},{3,1},{4,2},{5,3},{6,4},{7,5},{8,6},{9,7},{10,... | collective-permute-start | bytes 1572872 | tf_op jit(solution)/shard_map/ppermute | solution.py:34
  25.1 13.2 %collective-permute-start.1 = (f32[2,512,128]{2,1,0:T(8,128)S(1)}, f32[2,512,128]{2,1,0:T(8,128)S(1)}, u32[]{:S(2)}, u32[]{:S(2)}) collective-permute-start(f32[2,512,128]{2,1,0:T(8,128)S(1)} %pad_maximum_fusion.refs_2_), channel_id=1, source_target_pairs={{0,2},{1,3},{2,4},{3,5},{4,6},{5,7},{6,8},{7,9},{8,10},{9,11},{10,... | collective-permute-start | bytes 1572872 | tf_op jit(solution)/shard_map/ppermute | solution.py:34
  34.8 12.4 %collective-permute-start.4 = (f32[2,512,128]{2,1,0:T(8,128)S(1)}, f32[2,512,128]{2,1,0:T(8,128)S(1)}, u32[]{:S(2)}, u32[]{:S(2)}) collective-permute-start(f32[2,512,128]{2,1,0:T(8,128)S(1)} %collective-permute-done.2.refs_4_), channel_id=1, source_target_pairs={{0,14},{1,15},{2,0},{3,1},{4,2},{5,3},{6,4},{7,5},{8,6},{9,7},{10,... | collective-permute-start | bytes 1572872 | tf_op jit(solution)/shard_map/ppermute | solution.py:34
  38.3 12.3 %collective-permute-start.3 = (f32[2,512,128]{2,1,0:T(8,128)S(1)}, f32[2,512,128]{2,1,0:T(8,128)}, u32[]{:S(2)}, u32[]{:S(2)}) collective-permute-start(f32[2,512,128]{2,1,0:T(8,128)S(1)} %collective-permute-done.1.refs_3_), channel_id=1, source_target_pairs={{0,2},{1,3},{2,4},{3,5},{4,6},{5,7},{6,8},{7,9},{8,10},{9,11},{10,... | collective-permute-start | bytes 1572872 | tf_op jit(solution)/shard_map/ppermute | solution.py:34
  47.1 11.3 %collective-permute-start.6 = (f32[2,512,128]{2,1,0:T(8,128)S(1)}, f32[2,512,128]{2,1,0:T(8,128)S(1)}, u32[]{:S(2)}, u32[]{:S(2)}) collective-permute-start(f32[2,512,128]{2,1,0:T(8,128)S(1)} %collective-permute-done.4.refs_6_), channel_id=1, source_target_pairs={{0,14},{1,15},{2,0},{3,1},{4,2},{5,3},{6,4},{7,5},{8,6},{9,7},{10,... | collective-permute-start | bytes 1572872 | tf_op jit(solution)/shard_map/ppermute | solution.py:34
  50.6 12.2 %collective-permute-start.5 = (f32[2,512,128]{2,1,0:T(8,128)}, f32[2,512,128]{2,1,0:T(8,128)S(1)}, u32[]{:S(2)}, u32[]{:S(2)}) collective-permute-start(f32[2,512,128]{2,1,0:T(8,128)} %collective-permute-done.3.refs_5_), channel_id=1, source_target_pairs={{0,2},{1,3},{2,4},{3,5},{4,6},{5,7},{6,8},{7,9},{8,10},{9,11},{10,... | collective-permute-start | bytes 1572872 | tf_op jit(solution)/shard_map/ppermute | solution.py:34
  50.6 15.8 %collective-permute-start.9 = (f32[2,512,128]{2,1,0:T(8,128)S(1)}, f32[2,512,128]{2,1,0:T(8,128)S(1)}, u32[]{:S(2)}, u32[]{:S(2)}) collective-permute-start(f32[2,512,128]{2,1,0:T(8,128)S(1)} %pad_maximum_fusion.refs_2_), channel_id=1, source_target_pairs={{0,1},{1,0},{2,3},{3,2},{4,5},{5,4},{6,7},{7,6},{8,9},{9,8},{10,11... | collective-permute-start | bytes 1572872 | tf_op jit(solution)/shard_map/ppermute | solution.py:34
  54.1 13.1 %collective-permute-start.11 = (f32[2,512,128]{2,1,0:T(8,128)S(1)}, f32[2,512,128]{2,1,0:T(8,128)S(1)}, u32[]{:S(2)}, u32[]{:S(2)}) collective-permute-start(f32[2,512,128]{2,1,0:T(8,128)S(1)} %collective-permute-done.2.refs_4_), channel_id=1, source_target_pairs={{0,1},{1,0},{2,3},{3,2},{4,5},{5,4},{6,7},{7,6},{8,9},{9,8},{10,11... | collective-permute-start | bytes 1572872 | tf_op jit(solution)/shard_map/ppermute | solution.py:34
  54.2 15.2 %collective-permute-start.10 = (f32[2,512,128]{2,1,0:T(8,128)S(1)}, f32[2,512,128]{2,1,0:T(8,128)S(1)}, u32[]{:S(2)}, u32[]{:S(2)}) collective-permute-start(f32[2,512,128]{2,1,0:T(8,128)S(1)} %collective-permute-done.1.refs_3_), channel_id=1, source_target_pairs={{0,1},{1,0},{2,3},{3,2},{4,5},{5,4},{6,7},{7,6},{8,9},{9,8},{10,11... | collective-permute-start | bytes 1572872 | tf_op jit(solution)/shard_map/ppermute | solution.py:34
  58.5 12.3 %collective-permute-start.13 = (f32[2,512,128]{2,1,0:T(8,128)S(1)}, f32[2,512,128]{2,1,0:T(8,128)S(1)}, u32[]{:S(2)}, u32[]{:S(2)}) collective-permute-start(f32[2,512,128]{2,1,0:T(8,128)S(1)} %collective-permute-done.4.refs_6_), channel_id=1, source_target_pairs={{0,1},{1,0},{2,3},{3,2},{4,5},{5,4},{6,7},{7,6},{8,9},{9,8},{10,11... | collective-permute-start | bytes 1572872 | tf_op jit(solution)/shard_map/ppermute | solution.py:34
  62.7 15.4 %collective-permute-start.12 = (f32[2,512,128]{2,1,0:T(8,128)}, f32[2,512,128]{2,1,0:T(8,128)}, u32[]{:S(2)}, u32[]{:S(2)}) collective-permute-start(f32[2,512,128]{2,1,0:T(8,128)} %collective-permute-done.3.refs_5_), channel_id=1, source_target_pairs={{0,1},{1,0},{2,3},{3,2},{4,5},{5,4},{6,7},{7,6},{8,9},{9,8},{10,11... | collective-permute-start | bytes 1572872 | tf_op jit(solution)/shard_map/ppermute | solution.py:34
  137.2 11.1 %collective-permute-start.19 = (f32[2,512,128]{2,1,0:T(8,128)S(1)}, f32[2,512,128]{2,1,0:T(8,128)S(1)}, u32[]{:S(2)}, u32[]{:S(2)}) collective-permute-start(f32[2,512,128]{2,1,0:T(8,128)S(1)} %pad_maximum_fusion.1.refs_2_), channel_id=1, source_target_pairs={{0,2},{1,3},{2,4},{3,5},{4,6},{5,7},{6,8},{7,9},{8,10},{9,11},{10,... | collective-permute-start | bytes 1572872 | tf_op jit(solution)/shard_map/ppermute | solution.py:34
  146.7 10.5 %collective-permute-start.22 = (f32[2,512,128]{2,1,0:T(8,128)S(1)}, f32[2,512,128]{2,1,0:T(8,128)S(1)}, u32[]{:S(2)}, u32[]{:S(2)}) collective-permute-start(f32[2,512,128]{2,1,0:T(8,128)S(1)} %collective-permute-done.20.refs_4_), channel_id=1, source_target_pairs={{0,14},{1,15},{2,0},{3,1},{4,2},{5,3},{6,4},{7,5},{8,6},{9,7},{10,... | collective-permute-start | bytes 1572872 | tf_op jit(solution)/shard_map/ppermute | solution.py:34
  148.2 10.4 %collective-permute-start.21 = (f32[2,512,128]{2,1,0:T(8,128)S(1)}, f32[2,512,128]{2,1,0:T(8,128)S(1)}, u32[]{:S(2)}, u32[]{:S(2)}) collective-permute-start(f32[2,512,128]{2,1,0:T(8,128)S(1)} %collective-permute-done.19.refs_3_), channel_id=1, source_target_pairs={{0,2},{1,3},{2,4},{3,5},{4,6},{5,7},{6,8},{7,9},{8,10},{9,11},{10,... | collective-permute-start | bytes 1572872 | tf_op jit(solution)/shard_map/ppermute | solution.py:34
  157.2 10.8 %collective-permute-start.24 = (f32[2,512,128]{2,1,0:T(8,128)S(1)}, f32[2,512,128]{2,1,0:T(8,128)S(1)}, u32[]{:S(2)}, u32[]{:S(2)}) collective-permute-start(f32[2,512,128]{2,1,0:T(8,128)S(1)} %collective-permute-done.22.refs_6_), channel_id=1, source_target_pairs={{0,14},{1,15},{2,0},{3,1},{4,2},{5,3},{6,4},{7,5},{8,6},{9,7},{10,... | collective-permute-start | bytes 1572872 | tf_op jit(solution)/shard_map/ppermute | solution.py:34
  158.6 15.7 %collective-permute-start.23 = (f32[2,512,128]{2,1,0:T(8,128)S(1)}, f32[2,512,128]{2,1,0:T(8,128)S(1)}, u32[]{:S(2)}, u32[]{:S(2)}) collective-permute-start(f32[2,512,128]{2,1,0:T(8,128)S(1)} %collective-permute-done.21.refs_5_), channel_id=1, source_target_pairs={{0,2},{1,3},{2,4},{3,5},{4,6},{5,7},{6,8},{7,9},{8,10},{9,11},{10,... | collective-permute-start | bytes 1572872 | tf_op jit(solution)/shard_map/ppermute | solution.py:34
  158.7 16.9 %collective-permute-start.27 = (f32[2,512,128]{2,1,0:T(8,128)S(1)}, f32[2,512,128]{2,1,0:T(8,128)S(1)}, u32[]{:S(2)}, u32[]{:S(2)}) collective-permute-start(f32[2,512,128]{2,1,0:T(8,128)S(1)} %pad_maximum_fusion.1.refs_2_), channel_id=1, source_target_pairs={{0,1},{1,0},{2,3},{3,2},{4,5},{5,4},{6,7},{7,6},{8,9},{9,8},{10,11... | collective-permute-start | bytes 1572872 | tf_op jit(solution)/shard_map/ppermute | solution.py:34
  167.1 11.6 %collective-permute-start.28 = (f32[2,512,128]{2,1,0:T(8,128)S(1)}, f32[2,512,128]{2,1,0:T(8,128)S(1)}, u32[]{:S(2)}, u32[]{:S(2)}) collective-permute-start(f32[2,512,128]{2,1,0:T(8,128)S(1)} %collective-permute-done.19.refs_3_), channel_id=1, source_target_pairs={{0,1},{1,0},{2,3},{3,2},{4,5},{5,4},{6,7},{7,6},{8,9},{9,8},{10,11... | collective-permute-start | bytes 1572872 | tf_op jit(solution)/shard_map/ppermute | solution.py:34
  168.1 12.0 %collective-permute-start.31 = (f32[2,512,128]{2,1,0:T(8,128)S(1)}, f32[2,512,128]{2,1,0:T(8,128)S(1)}, u32[]{:S(2)}, u32[]{:S(2)}) collective-permute-start(f32[2,512,128]{2,1,0:T(8,128)S(1)} %collective-permute-done.22.refs_6_), channel_id=1, source_target_pairs={{0,1},{1,0},{2,3},{3,2},{4,5},{5,4},{6,7},{7,6},{8,9},{9,8},{10,11... | collective-permute-start | bytes 1572872 | tf_op jit(solution)/shard_map/ppermute | solution.py:34
  174.3 13.6 %collective-permute-start.30 = (f32[2,512,128]{2,1,0:T(8,128)S(1)}, f32[2,512,128]{2,1,0:T(8,128)S(1)}, u32[]{:S(2)}, u32[]{:S(2)}) collective-permute-start(f32[2,512,128]{2,1,0:T(8,128)S(1)} %collective-permute-done.21.refs_5_), channel_id=1, source_target_pairs={{0,1},{1,0},{2,3},{3,2},{4,5},{5,4},{6,7},{7,6},{8,9},{9,8},{10,11... | collective-permute-start | bytes 1572872 | tf_op jit(solution)/shard_map/ppermute | solution.py:34
  179.5 9.8 %collective-permute-start.33 = (f32[2,512,128]{2,1,0:T(8,128)S(1)}, f32[2,512,128]{2,1,0:T(8,128)S(1)}, u32[]{:S(2)}, u32[]{:S(2)}) collective-permute-start(f32[2,512,128]{2,1,0:T(8,128)S(1)} %collective-permute-done.24.refs_8_), channel_id=1, source_target_pairs={{0,1},{1,0},{2,3},{3,2},{4,5},{5,4},{6,7},{7,6},{8,9},{9,8},{10,11... | collective-permute-start | bytes 1572872 | tf_op jit(solution)/shard_map/ppermute | solution.py:34
  180.9 10.0 %collective-permute-start.32 = (f32[2,512,128]{2,1,0:T(8,128)S(1)}, f32[2,512,128]{2,1,0:T(8,128)S(1)}, u32[]{:S(2)}, u32[]{:S(2)}) collective-permute-start(f32[2,512,128]{2,1,0:T(8,128)S(1)} %collective-permute-done.23.refs_7_), channel_id=1, source_target_pairs={{0,1},{1,0},{2,3},{3,2},{4,5},{5,4},{6,7},{7,6},{8,9},{9,8},{10,11... | collective-permute-start | bytes 1572872 | tf_op jit(solution)/shard_map/ppermute | solution.py:34
  (46 other events, 160.6 us)
Sparse Core Ops, SparseCore 0:
  9.7 58.2 all-gather.2
  128.5 50.8 all-gather.4

commit v3 on v2

--- a/solution.py
+++ b/solution.py
@@ -61,20 +61,13 @@
     pieces = refs[: len(sizes)]
     panel = refs[len(sizes)]
     square = refs[len(sizes) + 1] if combine else None
-    out, held, total, sems = refs[-4:]
-    slot = 0
-    for piece, n in zip(pieces, sizes):
-        for j in range(n):
-            pltpu.make_async_copy(piece.at[j], held.at[slot], sems.at[slot]).start()
-            slot += 1
-    total[...] = jnp.zeros_like(total)
-
-    def step(g, carry):
+    out, total = refs[-2:]
+    slots = [(piece, j) for piece, n in zip(pieces, sizes) for j in range(n)]
+    for g in range(0, len(slots), GROUP):
         left, right = [], []
-        for q in range(GROUP):
-            s = g * GROUP + q
-            pltpu.make_async_copy(held.at[s], held.at[s], sems.at[s]).wait()
-            left.append(held[s])
+        for s in range(g, g + GROUP):
+            piece, j = slots[s]
+            left.append(piece[j])
             right.append(panel[pl.ds(pl.multiple_of(columns[s] * BLK, BLK), BLK), :])
         left_high, left_low = split(jnp.concatenate(left, axis=1))
         right_high, right_low = split(jnp.concatenate(right, axis=0))
@@ -84,10 +77,8 @@
             preferred_element_type=jnp.float32,
         )
         narrow = jnp.dot(left_low, right_high, preferred_element_type=jnp.float32)
-        total[...] += (wide[:, BLK:] + narrow) + wide[:, :BLK]
-        return carry
-
-    lax.fori_loop(0, held.shape[0] // GROUP, step, 0)
+        term = (wide[:, BLK:] + narrow) + wide[:, :BLK]
+        total[...] = term if g == 0 else total[...] + term
     for i in range(out.shape[0] // BLK):
         rows = pl.ds(i * BLK, BLK)
         masked = live[i] * total[rows, :]
@@ -105,16 +96,10 @@
     return pl.pallas_call(
         body,
         out_shape=jax.ShapeDtypeStruct((rows, BLK), jnp.float32),
-        in_specs=[smem, smem]
-        + [pl.BlockSpec(memory_space=pl.ANY)] * len(pieces)
-        + [vmem] * (2 if combine else 1),
+        in_specs=[smem, smem] + [vmem] * (len(pieces) + (2 if combine else 1)),
         out_specs=vmem,
-        scratch_shapes=[
-            pltpu.VMEM((slots, rows, BLK), jnp.float32),
-            pltpu.VMEM((rows, BLK), jnp.float32),
-            pltpu.SemaphoreType.DMA((slots,)),
-        ],
-        compiler_params=pltpu.CompilerParams(vmem_limit_bytes=32 << 20),
+        scratch_shapes=[pltpu.VMEM((rows, BLK), jnp.float32)],
+        compiler_params=pltpu.CompilerParams(vmem_limit_bytes=24 << 20),
         cost_estimate=pl.CostEstimate(
             flops=6 * rows * slots * BLK * BLK,
             bytes_accessed=4 * BLK * (slots * (rows + BLK) + 2 * rows),

time: 256 us -> 249 us (0.973)
  Pallas kernels: 23.7 us -> 15.5 us
    pallas_call x4, Pallas kernels: 23.7 us -> 15.5 us  [product(): pl.pallas_call(body, out_shape=jax.ShapeDtypeStruct((rows, BLK), jnp.floa...]
where the time goes in v3:
time: 249 us; the launch traced here: 248 us
  blocking collectives  63.6 us (26%)
  starting transfers between devices  60.2 us (24%)
  waiting for transfers between devices  59.8 us (24%)
  local copies, waits for them, and re-layouts  30.1 us (12%)
  Pallas kernels  15.5 us (6%)
  between operations  13.6 us (5%)
  other arithmetic  4.89 us (2%)
    all_to_all x2, blocking collectives, gather_rows(): got = lax.all_to_all(copies, name, 0, 0)  63.6 us
    ppermute x36, starting transfers between devices, gather_cols(): send = lambda v, pairs: lax.ppermute(v, 'col', pairs)  60.1 us
    ppermute x36, waiting for transfers between devices, gather_cols(): send = lambda v, pairs: lax.ppermute(v, 'col', pairs)  59.7 us
    unnamed x65, local copies, waits for them, and re-layouts  29.5 us
    pallas_call x4, Pallas kernels, product(): pl.pallas_call(body, out_shape=jax.ShapeDtypeStruct((rows, BLK), jnp.floa...  15.5 us
  transfers between devices with their start and end apart: 38, of which 13 were waited for; matrix products, arithmetic and copies ran while one was open for 1% of the time, Pallas kernels for 0%

profile of v3, /device:TPU:1, one launch (start us, length us, event | category | flops | bytes accessed | tf_op | source)
XLA Modules:
  0.0 247.7 jit_solution(9481159061878084525)
XLA Ops:
  9.6 3.7 %collective-permute-start = (f32[512,128]{1,0:T(8,128)}, f32[512,128]{1,0:T(8,128)S(1)}, u32[]{:S(2)}, u32[]{:S(2)}) collective-permute-start(f32[512,128]{1,0:T(8,128)} %multiply_add_fusion), channel_id=1, source_target_pairs={{0,16},{1,17},{2,18},{3,19},{4,20},{5,21},{6,22},{7,23},{8,24},{9,... | collective-permute-start | bytes 786440 | tf_op jit(solution)/shard_map/ppermute | solution.py:34
  14.4 4.1 %collective-permute-done = f32[512,128]{1,0:T(8,128)S(1)} collective-permute-done((f32[512,128]{1,0:T(8,128)}, f32[512,128]{1,0:T(8,128)S(1)}, u32[]{:S(2)}, u32[]{:S(2)}) %collective-permute-start) | collective-permute-done | bytes 262176 | tf_op jit(solution)/shard_map/ppermute | solution.py:34
  18.6 6.5 %collective-permute-start.2 = (f32[2,512,128]{2,1,0:T(8,128)S(1)}, f32[2,512,128]{2,1,0:T(8,128)S(1)}, u32[]{:S(2)}, u32[]{:S(2)}) collective-permute-start(f32[2,512,128]{2,1,0:T(8,128)S(1)} %pad_maximum_fusion.refs_2_), channel_id=1, source_target_pairs={{0,14},{1,15},{2,0},{3,1},{4,2},{5,3},{6,4},{7,5},{8,6},{9,7},{10,... | collective-permute-start | bytes 1572872 | tf_op jit(solution)/shard_map/ppermute | solution.py:34
  25.1 9.7 %collective-permute-done.2.refs_4_ = f32[2,512,128]{2,1,0:T(8,128)S(1)} collective-permute-done((f32[2,512,128]{2,1,0:T(8,128)S(1)}, f32[2,512,128]{2,1,0:T(8,128)S(1)}, u32[]{:S(2)}, u32[]{:S(2)}) %collective-permute-start.2) | collective-permute-done | bytes 524320 | tf_op jit(solution)/shard_map/ppermute | solution.py:34
  34.8 3.5 %collective-permute-start.4 = (f32[2,512,128]{2,1,0:T(8,128)S(1)}, f32[2,512,128]{2,1,0:T(8,128)S(1)}, u32[]{:S(2)}, u32[]{:S(2)}) collective-permute-start(f32[2,512,128]{2,1,0:T(8,128)S(1)} %collective-permute-done.2.refs_4_), channel_id=1, source_target_pairs={{0,14},{1,15},{2,0},{3,1},{4,2},{5,3},{6,4},{7,5},{8,6},{9,7},{10,... | collective-permute-start | bytes 1572872 | tf_op jit(solution)/shard_map/ppermute | solution.py:34
  38.3 8.8 %collective-permute-done.4.refs_6_ = f32[2,512,128]{2,1,0:T(8,128)S(1)} collective-permute-done((f32[2,512,128]{2,1,0:T(8,128)S(1)}, f32[2,512,128]{2,1,0:T(8,128)S(1)}, u32[]{:S(2)}, u32[]{:S(2)}) %collective-permute-start.4) | collective-permute-done | bytes 524320 | tf_op jit(solution)/shard_map/ppermute | solution.py:34
  47.1 3.4 %collective-permute-start.6 = (f32[2,512,128]{2,1,0:T(8,128)S(1)}, f32[2,512,128]{2,1,0:T(8,128)S(1)}, u32[]{:S(2)}, u32[]{:S(2)}) collective-permute-start(f32[2,512,128]{2,1,0:T(8,128)S(1)} %collective-permute-done.4.refs_6_), channel_id=1, source_target_pairs={{0,14},{1,15},{2,0},{3,1},{4,2},{5,3},{6,4},{7,5},{8,6},{9,7},{10,... | collective-permute-start | bytes 1572872 | tf_op jit(solution)/shard_map/ppermute | solution.py:34
  50.6 3.6 %collective-permute-start.9 = (f32[2,512,128]{2,1,0:T(8,128)S(1)}, f32[2,512,128]{2,1,0:T(8,128)S(1)}, u32[]{:S(2)}, u32[]{:S(2)}) collective-permute-start(f32[2,512,128]{2,1,0:T(8,128)S(1)} %pad_maximum_fusion.refs_2_), channel_id=1, source_target_pairs={{0,1},{1,0},{2,3},{3,2},{4,5},{5,4},{6,7},{7,6},{8,9},{9,8},{10,11... | collective-permute-start | bytes 1572872 | tf_op jit(solution)/shard_map/ppermute | solution.py:34
  54.6 3.8 %collective-permute-done.6.refs_8_ = f32[2,512,128]{2,1,0:T(8,128)S(1)} collective-permute-done((f32[2,512,128]{2,1,0:T(8,128)S(1)}, f32[2,512,128]{2,1,0:T(8,128)S(1)}, u32[]{:S(2)}, u32[]{:S(2)}) %collective-permute-start.6) | collective-permute-done | bytes 524320 | tf_op jit(solution)/shard_map/ppermute | solution.py:34
  58.5 4.2 %collective-permute-start.13 = (f32[2,512,128]{2,1,0:T(8,128)S(1)}, f32[2,512,128]{2,1,0:T(8,128)S(1)}, u32[]{:S(2)}, u32[]{:S(2)}) collective-permute-start(f32[2,512,128]{2,1,0:T(8,128)S(1)} %collective-permute-done.4.refs_6_), channel_id=1, source_target_pairs={{0,1},{1,0},{2,3},{3,2},{4,5},{5,4},{6,7},{7,6},{8,9},{9,8},{10,11... | collective-permute-start | bytes 1572872 | tf_op jit(solution)/shard_map/ppermute | solution.py:34
  62.7 3.6 %collective-permute-start.12 = (f32[2,512,128]{2,1,0:T(8,128)}, f32[2,512,128]{2,1,0:T(8,128)}, u32[]{:S(2)}, u32[]{:S(2)}) collective-permute-start(f32[2,512,128]{2,1,0:T(8,128)} %collective-permute-done.3.refs_5_), channel_id=1, source_target_pairs={{0,1},{1,0},{2,3},{3,2},{4,5},{5,4},{6,7},{7,6},{8,9},{9,8},{10,11... | collective-permute-start | bytes 1572872 | tf_op jit(solution)/shard_map/ppermute | solution.py:34
  71.6 3.6 %collective-permute-done.8.refs_10_ = f32[1,512,128]{2,1,0:T(8,128)S(1)} collective-permute-done((f32[1,512,128]{2,1,0:T(8,128)S(1)}, f32[1,512,128]{2,1,0:T(8,128)S(1)}, u32[]{:S(2)}, u32[]{:S(2)}) %collective-permute-start.8) | collective-permute-done | bytes 262176 | tf_op jit(solution)/shard_map/ppermute | solution.py:34
  85.3 4.1 %shard_map.28.refs_21_ = f32[512,128]{1,0:T(8,128)S(1)} custom-call(s32[32]{0:T(128)S(1)} %stack.149.refs_0_, f32[4]{0:T(128)S(1)} %get-tuple-element.6.refs_1_, f32[2,512,128]{2,1,0:T(8,128)S(1)} %pad_maximum_fusion.refs_2_, f32[2,512,128]{2,1,0:T(8,128)S(1)} %collective-permute-done.1.refs_3_, f32[2,512,128]{2,1,0:T(8,128)S(1)} %collective-permute-done.2.refs_4_, ...), custom_call_target="tpu_custom_call" | custom-call | flops 1610612736 | bytes 11010048 | tf_op jit(solution)/shard_map/pallas_call | solution.py:96
  89.6 30.8 %all_to_all.10 = f32[8,512,128]{2,1,0:T(8,128)S(1)} all-to-all(f32[8,512,128]{2,1,0:T(8,128)S(1)} %broadcast_in_dim.7), channel_id=1, replica_groups=mesh['row'=8,'col'=32] {'row'}, dimensions={0} | all-to-all | bytes 4194304 | tf_op jit(solution)/shard_map/all_to_all | solution.py:18
  120.4 4.8 %shard_map.29 = f32[512,128]{1,0:T(8,128)} custom-call(s32[32]{0:T(128)S(1)} %stack.149.refs_0_, f32[4]{0:T(128)S(1)} %get-tuple-element.6.refs_1_, f32[2,512,128]{2,1,0:T(8,128)S(1)} %pad_maximum_fusion.refs_2_, f32[2,512,128]{2,1,0:T(8,128)S(1)} %collective-permute-done.1.refs_3_, f32[2,512,128]{2,1,0:T(8,128)S(1)} %collective-permute-done.2.refs_4_, ...), custom_call_target="tpu_custom_call" | custom-call | flops 1610612736 | bytes 11010048 | tf_op jit(solution)/shard_map/pallas_call | solution.py:96
  127.9 5.2 %collective-permute-done.18 = f32[512,128]{1,0:T(8,128)S(1)} collective-permute-done((f32[512,128]{1,0:T(8,128)}, f32[512,128]{1,0:T(8,128)S(1)}, u32[]{:S(2)}, u32[]{:S(2)}) %collective-permute-start.18) | collective-permute-done | bytes 262176 | tf_op jit(solution)/shard_map/ppermute | solution.py:34
  135.6 8.6 %collective-permute-done.20.refs_4_ = f32[2,512,128]{2,1,0:T(8,128)S(1)} collective-permute-done((f32[2,512,128]{2,1,0:T(8,128)S(1)}, f32[2,512,128]{2,1,0:T(8,128)S(1)}, u32[]{:S(2)}, u32[]{:S(2)}) %collective-permute-start.20) | collective-permute-done | bytes 524320 | tf_op jit(solution)/shard_map/ppermute | solution.py:34
  145.7 9.0 %collective-permute-done.22.refs_6_ = f32[2,512,128]{2,1,0:T(8,128)S(1)} collective-permute-done((f32[2,512,128]{2,1,0:T(8,128)S(1)}, f32[2,512,128]{2,1,0:T(8,128)S(1)}, u32[]{:S(2)}, u32[]{:S(2)}) %collective-permute-start.22) | collective-permute-done | bytes 524320 | tf_op jit(solution)/shard_map/ppermute | solution.py:34
  156.4 7.2 %collective-permute-start.27 = (f32[2,512,128]{2,1,0:T(8,128)S(1)}, f32[2,512,128]{2,1,0:T(8,128)S(1)}, u32[]{:S(2)}, u32[]{:S(2)}) collective-permute-start(f32[2,512,128]{2,1,0:T(8,128)S(1)} %pad_maximum_fusion.1.refs_2_), channel_id=1, source_target_pairs={{0,1},{1,0},{2,3},{3,2},{4,5},{5,4},{6,7},{7,6},{8,9},{9,8},{10,11... | collective-permute-start | bytes 1572872 | tf_op jit(solution)/shard_map/ppermute | solution.py:34
  165.1 5.8 %collective-permute-start.31 = (f32[2,512,128]{2,1,0:T(8,128)S(1)}, f32[2,512,128]{2,1,0:T(8,128)S(1)}, u32[]{:S(2)}, u32[]{:S(2)}) collective-permute-start(f32[2,512,128]{2,1,0:T(8,128)S(1)} %collective-permute-done.22.refs_6_), channel_id=1, source_target_pairs={{0,1},{1,0},{2,3},{3,2},{4,5},{5,4},{6,7},{7,6},{8,9},{9,8},{10,11... | collective-permute-start | bytes 1572872 | tf_op jit(solution)/shard_map/ppermute | solution.py:34
  177.7 3.5 %collective-permute-done.26.refs_10_ = f32[1,512,128]{2,1,0:T(8,128)S(1)} collective-permute-done((f32[1,512,128]{2,1,0:T(8,128)S(1)}, f32[1,512,128]{2,1,0:T(8,128)S(1)}, u32[]{:S(2)}, u32[]{:S(2)}) %collective-permute-start.26) | collective-permute-done | bytes 262176 | tf_op jit(solution)/shard_map/ppermute | solution.py:34
  201.4 2.9 %shard_map.30.refs_21_ = f32[512,128]{1,0:T(8,128)S(1)} custom-call(s32[32]{0:T(128)S(1)} %stack.149.refs_0_, f32[4]{0:T(128)S(1)} %get-tuple-element.6.refs_1_, f32[2,512,128]{2,1,0:T(8,128)S(1)} %pad_maximum_fusion.1.refs_2_, f32[2,512,128]{2,1,0:T(8,128)S(1)} %collective-permute-done.19.refs_3_, f32[2,512,128]{2,1,0:T(8,128)S(1)} %collective-permute-done.20.refs_4_, ...), custom_call_target="tpu_custom_call" | custom-call | flops 1610612736 | bytes 11010048 | tf_op jit(solution)/shard_map/pallas_call | solution.py:96
  204.5 32.8 %all_to_all.11 = f32[8,512,128]{2,1,0:T(8,128)S(1)} all-to-all(f32[8,512,128]{2,1,0:T(8,128)S(1)} %broadcast_in_dim.8), channel_id=1, replica_groups=mesh['row'=8,'col'=32] {'row'}, dimensions={0} | all-to-all | bytes 4194304 | tf_op jit(solution)/shard_map/all_to_all | solution.py:18
  237.3 3.6 %shard_map.31 = f32[512,128]{1,0:T(8,128)} custom-call(s32[32]{0:T(128)S(1)} %stack.149.refs_0_, f32[4]{0:T(128)S(1)} %get-tuple-element.6.refs_1_, f32[2,512,128]{2,1,0:T(8,128)S(1)} %pad_maximum_fusion.1.refs_2_, f32[2,512,128]{2,1,0:T(8,128)S(1)} %collective-permute-done.19.refs_3_, f32[2,512,128]{2,1,0:T(8,128)S(1)} %collective-permute-done.20.refs_4_, ...), custom_call_target="tpu_custom_call" | custom-call | flops 1610612736 | bytes 11010048 | tf_op jit(solution)/shard_map/pallas_call | solution.py:96
  (143 shorter events, 57.2 us)
Async XLA Ops:
  6.5 73.0 %all-gather.3.cloned.1.call-start = ((), (), s32[]{:S(2)}) async-start(), calls=%async_computation.2 | async-start | bytes 2359296 | tf_op jit(solution)/shard_map/all_gather | solution.py:131
  9.6 179.1 %all-gather.5.cloned.1.call-start = ((), (), s32[]{:S(2)}) async-start(), calls=%async_computation.3 | async-start | bytes 2359296 | tf_op jit(solution)/shard_map/all_gather | solution.py:131
  18.6 16.2 %collective-permute-start.2 = (f32[2,512,128]{2,1,0:T(8,128)S(1)}, f32[2,512,128]{2,1,0:T(8,128)S(1)}, u32[]{:S(2)}, u32[]{:S(2)}) collective-permute-start(f32[2,512,128]{2,1,0:T(8,128)S(1)} %pad_maximum_fusion.refs_2_), channel_id=1, source_target_pairs={{0,14},{1,15},{2,0},{3,1},{4,2},{5,3},{6,4},{7,5},{8,6},{9,7},{10,... | collective-permute-start | bytes 1572872 | tf_op jit(solution)/shard_map/ppermute | solution.py:34
  25.1 13.2 %collective-permute-start.1 = (f32[2,512,128]{2,1,0:T(8,128)S(1)}, f32[2,512,128]{2,1,0:T(8,128)S(1)}, u32[]{:S(2)}, u32[]{:S(2)}) collective-permute-start(f32[2,512,128]{2,1,0:T(8,128)S(1)} %pad_maximum_fusion.refs_2_), channel_id=1, source_target_pairs={{0,2},{1,3},{2,4},{3,5},{4,6},{5,7},{6,8},{7,9},{8,10},{9,11},{10,... | collective-permute-start | bytes 1572872 | tf_op jit(solution)/shard_map/ppermute | solution.py:34
  34.8 12.4 %collective-permute-start.4 = (f32[2,512,128]{2,1,0:T(8,128)S(1)}, f32[2,512,128]{2,1,0:T(8,128)S(1)}, u32[]{:S(2)}, u32[]{:S(2)}) collective-permute-start(f32[2,512,128]{2,1,0:T(8,128)S(1)} %collective-permute-done.2.refs_4_), channel_id=1, source_target_pairs={{0,14},{1,15},{2,0},{3,1},{4,2},{5,3},{6,4},{7,5},{8,6},{9,7},{10,... | collective-permute-start | bytes 1572872 | tf_op jit(solution)/shard_map/ppermute | solution.py:34
  38.3 12.3 %collective-permute-start.3 = (f32[2,512,128]{2,1,0:T(8,128)S(1)}, f32[2,512,128]{2,1,0:T(8,128)}, u32[]{:S(2)}, u32[]{:S(2)}) collective-permute-start(f32[2,512,128]{2,1,0:T(8,128)S(1)} %collective-permute-done.1.refs_3_), channel_id=1, source_target_pairs={{0,2},{1,3},{2,4},{3,5},{4,6},{5,7},{6,8},{7,9},{8,10},{9,11},{10,... | collective-permute-start | bytes 1572872 | tf_op jit(solution)/shard_map/ppermute | solution.py:34
  47.1 11.3 %collective-permute-start.6 = (f32[2,512,128]{2,1,0:T(8,128)S(1)}, f32[2,512,128]{2,1,0:T(8,128)S(1)}, u32[]{:S(2)}, u32[]{:S(2)}) collective-permute-start(f32[2,512,128]{2,1,0:T(8,128)S(1)} %collective-permute-done.4.refs_6_), channel_id=1, source_target_pairs={{0,14},{1,15},{2,0},{3,1},{4,2},{5,3},{6,4},{7,5},{8,6},{9,7},{10,... | collective-permute-start | bytes 1572872 | tf_op jit(solution)/shard_map/ppermute | solution.py:34
  50.6 12.2 %collective-permute-start.5 = (f32[2,512,128]{2,1,0:T(8,128)}, f32[2,512,128]{2,1,0:T(8,128)S(1)}, u32[]{:S(2)}, u32[]{:S(2)}) collective-permute-start(f32[2,512,128]{2,1,0:T(8,128)} %collective-permute-done.3.refs_5_), channel_id=1, source_target_pairs={{0,2},{1,3},{2,4},{3,5},{4,6},{5,7},{6,8},{7,9},{8,10},{9,11},{10,... | collective-permute-start | bytes 1572872 | tf_op jit(solution)/shard_map/ppermute | solution.py:34
  50.6 15.8 %collective-permute-start.9 = (f32[2,512,128]{2,1,0:T(8,128)S(1)}, f32[2,512,128]{2,1,0:T(8,128)S(1)}, u32[]{:S(2)}, u32[]{:S(2)}) collective-permute-start(f32[2,512,128]{2,1,0:T(8,128)S(1)} %pad_maximum_fusion.refs_2_), channel_id=1, source_target_pairs={{0,1},{1,0},{2,3},{3,2},{4,5},{5,4},{6,7},{7,6},{8,9},{9,8},{10,11... | collective-permute-start | bytes 1572872 | tf_op jit(solution)/shard_map/ppermute | solution.py:34
  54.1 13.1 %collective-permute-start.11 = (f32[2,512,128]{2,1,0:T(8,128)S(1)}, f32[2,512,128]{2,1,0:T(8,128)S(1)}, u32[]{:S(2)}, u32[]{:S(2)}) collective-permute-start(f32[2,512,128]{2,1,0:T(8,128)S(1)} %collective-permute-done.2.refs_4_), channel_id=1, source_target_pairs={{0,1},{1,0},{2,3},{3,2},{4,5},{5,4},{6,7},{7,6},{8,9},{9,8},{10,11... | collective-permute-start | bytes 1572872 | tf_op jit(solution)/shard_map/ppermute | solution.py:34
  54.2 15.2 %collective-permute-start.10 = (f32[2,512,128]{2,1,0:T(8,128)S(1)}, f32[2,512,128]{2,1,0:T(8,128)S(1)}, u32[]{:S(2)}, u32[]{:S(2)}) collective-permute-start(f32[2,512,128]{2,1,0:T(8,128)S(1)} %collective-permute-done.1.refs_3_), channel_id=1, source_target_pairs={{0,1},{1,0},{2,3},{3,2},{4,5},{5,4},{6,7},{7,6},{8,9},{9,8},{10,11... | collective-permute-start | bytes 1572872 | tf_op jit(solution)/shard_map/ppermute | solution.py:34
  58.5 12.3 %collective-permute-start.13 = (f32[2,512,128]{2,1,0:T(8,128)S(1)}, f32[2,512,128]{2,1,0:T(8,128)S(1)}, u32[]{:S(2)}, u32[]{:S(2)}) collective-permute-start(f32[2,512,128]{2,1,0:T(8,128)S(1)} %collective-permute-done.4.refs_6_), channel_id=1, source_target_pairs={{0,1},{1,0},{2,3},{3,2},{4,5},{5,4},{6,7},{7,6},{8,9},{9,8},{10,11... | collective-permute-start | bytes 1572872 | tf_op jit(solution)/shard_map/ppermute | solution.py:34
  62.7 15.4 %collective-permute-start.12 = (f32[2,512,128]{2,1,0:T(8,128)}, f32[2,512,128]{2,1,0:T(8,128)}, u32[]{:S(2)}, u32[]{:S(2)}) collective-permute-start(f32[2,512,128]{2,1,0:T(8,128)} %collective-permute-done.3.refs_5_), channel_id=1, source_target_pairs={{0,1},{1,0},{2,3},{3,2},{4,5},{5,4},{6,7},{7,6},{8,9},{9,8},{10,11... | collective-permute-start | bytes 1572872 | tf_op jit(solution)/shard_map/ppermute | solution.py:34
  134.0 10.1 %collective-permute-start.20 = (f32[2,512,128]{2,1,0:T(8,128)S(1)}, f32[2,512,128]{2,1,0:T(8,128)S(1)}, u32[]{:S(2)}, u32[]{:S(2)}) collective-permute-start(f32[2,512,128]{2,1,0:T(8,128)S(1)} %pad_maximum_fusion.1.refs_2_), channel_id=1, source_target_pairs={{0,14},{1,15},{2,0},{3,1},{4,2},{5,3},{6,4},{7,5},{8,6},{9,7},{10,... | collective-permute-start | bytes 1572872 | tf_op jit(solution)/shard_map/ppermute | solution.py:34
  134.1 11.5 %collective-permute-start.19 = (f32[2,512,128]{2,1,0:T(8,128)S(1)}, f32[2,512,128]{2,1,0:T(8,128)S(1)}, u32[]{:S(2)}, u32[]{:S(2)}) collective-permute-start(f32[2,512,128]{2,1,0:T(8,128)S(1)} %pad_maximum_fusion.1.refs_2_), channel_id=1, source_target_pairs={{0,2},{1,3},{2,4},{3,5},{4,6},{5,7},{6,8},{7,9},{8,10},{9,11},{10,... | collective-permute-start | bytes 1572872 | tf_op jit(solution)/shard_map/ppermute | solution.py:34
  144.1 10.5 %collective-permute-start.22 = (f32[2,512,128]{2,1,0:T(8,128)S(1)}, f32[2,512,128]{2,1,0:T(8,128)S(1)}, u32[]{:S(2)}, u32[]{:S(2)}) collective-permute-start(f32[2,512,128]{2,1,0:T(8,128)S(1)} %collective-permute-done.20.refs_4_), channel_id=1, source_target_pairs={{0,14},{1,15},{2,0},{3,1},{4,2},{5,3},{6,4},{7,5},{8,6},{9,7},{10,... | collective-permute-start | bytes 1572872 | tf_op jit(solution)/shard_map/ppermute | solution.py:34
  145.7 10.7 %collective-permute-start.21 = (f32[2,512,128]{2,1,0:T(8,128)S(1)}, f32[2,512,128]{2,1,0:T(8,128)S(1)}, u32[]{:S(2)}, u32[]{:S(2)}) collective-permute-start(f32[2,512,128]{2,1,0:T(8,128)S(1)} %collective-permute-done.19.refs_3_), channel_id=1, source_target_pairs={{0,2},{1,3},{2,4},{3,5},{4,6},{5,7},{6,8},{7,9},{8,10},{9,11},{10,... | collective-permute-start | bytes 1572872 | tf_op jit(solution)/shard_map/ppermute | solution.py:34
  154.6 10.5 %collective-permute-start.24 = (f32[2,512,128]{2,1,0:T(8,128)S(1)}, f32[2,512,128]{2,1,0:T(8,128)S(1)}, u32[]{:S(2)}, u32[]{:S(2)}) collective-permute-start(f32[2,512,128]{2,1,0:T(8,128)S(1)} %collective-permute-done.22.refs_6_), channel_id=1, source_target_pairs={{0,14},{1,15},{2,0},{3,1},{4,2},{5,3},{6,4},{7,5},{8,6},{9,7},{10,... | collective-permute-start | bytes 1572872 | tf_op jit(solution)/shard_map/ppermute | solution.py:34
  156.4 14.6 %collective-permute-start.23 = (f32[2,512,128]{2,1,0:T(8,128)S(1)}, f32[2,512,128]{2,1,0:T(8,128)S(1)}, u32[]{:S(2)}, u32[]{:S(2)}) collective-permute-start(f32[2,512,128]{2,1,0:T(8,128)S(1)} %collective-permute-done.21.refs_5_), channel_id=1, source_target_pairs={{0,2},{1,3},{2,4},{3,5},{4,6},{5,7},{6,8},{7,9},{8,10},{9,11},{10,... | collective-permute-start | bytes 1572872 | tf_op jit(solution)/shard_map/ppermute | solution.py:34
  156.4 16.1 %collective-permute-start.27 = (f32[2,512,128]{2,1,0:T(8,128)S(1)}, f32[2,512,128]{2,1,0:T(8,128)S(1)}, u32[]{:S(2)}, u32[]{:S(2)}) collective-permute-start(f32[2,512,128]{2,1,0:T(8,128)S(1)} %pad_maximum_fusion.1.refs_2_), channel_id=1, source_target_pairs={{0,1},{1,0},{2,3},{3,2},{4,5},{5,4},{6,7},{7,6},{8,9},{9,8},{10,11... | collective-permute-start | bytes 1572872 | tf_op jit(solution)/shard_map/ppermute | solution.py:34
  163.6 11.9 %collective-permute-start.28 = (f32[2,512,128]{2,1,0:T(8,128)S(1)}, f32[2,512,128]{2,1,0:T(8,128)S(1)}, u32[]{:S(2)}, u32[]{:S(2)}) collective-permute-start(f32[2,512,128]{2,1,0:T(8,128)S(1)} %collective-permute-done.19.refs_3_), channel_id=1, source_target_pairs={{0,1},{1,0},{2,3},{3,2},{4,5},{5,4},{6,7},{7,6},{8,9},{9,8},{10,11... | collective-permute-start | bytes 1572872 | tf_op jit(solution)/shard_map/ppermute | solution.py:34
  165.1 11.8 %collective-permute-start.31 = (f32[2,512,128]{2,1,0:T(8,128)S(1)}, f32[2,512,128]{2,1,0:T(8,128)S(1)}, u32[]{:S(2)}, u32[]{:S(2)}) collective-permute-start(f32[2,512,128]{2,1,0:T(8,128)S(1)} %collective-permute-done.22.refs_6_), channel_id=1, source_target_pairs={{0,1},{1,0},{2,3},{3,2},{4,5},{5,4},{6,7},{7,6},{8,9},{9,8},{10,11... | collective-permute-start | bytes 1572872 | tf_op jit(solution)/shard_map/ppermute | solution.py:34
  171.0 13.9 %collective-permute-start.30 = (f32[2,512,128]{2,1,0:T(8,128)S(1)}, f32[2,512,128]{2,1,0:T(8,128)S(1)}, u32[]{:S(2)}, u32[]{:S(2)}) collective-permute-start(f32[2,512,128]{2,1,0:T(8,128)S(1)} %collective-permute-done.21.refs_5_), channel_id=1, source_target_pairs={{0,1},{1,0},{2,3},{3,2},{4,5},{5,4},{6,7},{7,6},{8,9},{9,8},{10,11... | collective-permute-start | bytes 1572872 | tf_op jit(solution)/shard_map/ppermute | solution.py:34
  177.7 10.1 %collective-permute-start.32 = (f32[2,512,128]{2,1,0:T(8,128)S(1)}, f32[2,512,128]{2,1,0:T(8,128)S(1)}, u32[]{:S(2)}, u32[]{:S(2)}) collective-permute-start(f32[2,512,128]{2,1,0:T(8,128)S(1)} %collective-permute-done.23.refs_7_), channel_id=1, source_target_pairs={{0,1},{1,0},{2,3},{3,2},{4,5},{5,4},{6,7},{7,6},{8,9},{9,8},{10,11... | collective-permute-start | bytes 1572872 | tf_op jit(solution)/shard_map/ppermute | solution.py:34
  (46 other events, 160.8 us)
Sparse Core Ops, SparseCore 0:
  9.7 58.2 all-gather.2
  125.4 50.9 all-gather.4

commit v4 on v1

v4 whole, which is shorter than its diff:
```python
import jax
import jax.numpy as jnp
from jax import lax
from jax.experimental import pallas as pl
from jax.experimental.pallas import tpu as pltpu
from jax.sharding import PartitionSpec as P

BLK = 128
NNZ = 6
ITERS = 2
X_HI, Z, CORE = 2, 8, 2
GROUP = 4


def col_id(x_hi, z, core):
    return (x_hi * Z + z % Z) * CORE + core


COLS = [(x, z, c) for x in range(X_HI) for z in range(Z) for c in range(CORE)]
UP = [(col_id(x, z, c), col_id(x, z + 1, c)) for x, z, c in COLS]
DOWN = [(col_id(x, z, c), col_id(x, z - 1, c)) for x, z, c in COLS]
ACROSS = [(col_id(x, z, c), col_id(1 - x, z, c)) for x, z, c in COLS]
TWIN = [(col_id(x, z, c), col_id(x, z, 1 - c)) for x, z, c in COLS]


def send(v, pairs):
    return lax.ppermute(v, "col", pairs)


def gather_rows(tile, name):
    parts = lax.axis_size(name)
    copies = jnp.broadcast_to(tile[None], (parts,) + tile.shape)
    got = lax.all_to_all(copies, name, 0, 0)
    return got.reshape(parts * tile.shape[0], tile.shape[1])


def gather_cols(tile):
    both = jnp.stack([tile, send(tile, ACROSS)])
    up = down = both
    pieces = [both]
    for _ in range(3):
        up, down = send(up, UP), send(down, DOWN)
        pieces += [up, down]
    return pieces + [send(up[:1], UP), send(down[1:], DOWN)]


def piece_columns(col):
    x_hi, z, core = col // (Z * CORE), (col // CORE) % Z, col % CORE
    away = jnp.array([0, 0, -1, -1, 1, 1, -2, -2, 2, 2, -3, -3, 3, 3, 4, 4], jnp.int32)
    across = jnp.arange(X_HI * Z, dtype=jnp.int32) % X_HI
    places = (x_hi + across) % X_HI * Z + (z + away + Z) % Z
    return jnp.concatenate([places, core[None].astype(jnp.int32)])


def to_pair(tile, core):
    rows = tile.reshape(-1, CORE, BLK, BLK)
    mine = jnp.where(core == 0, rows[:, 0], rows[:, 1])
    other = send(jnp.where(core == 0, rows[:, 1], rows[:, 0]), TWIN)
    left = jnp.where(core == 0, mine, other)
    right = jnp.where(core == 0, other, mine)
    return jnp.concatenate([left, right], axis=2).reshape(-1, CORE * BLK)


def split(x):
    high = x.astype(jnp.bfloat16)
    return high, (x - high.astype(jnp.float32)).astype(jnp.bfloat16)


def partial_product(sizes, where, pieces, panel, total):
    slots = [(piece, j) for piece, n in zip(pieces, sizes) for j in range(n)]
    for g in range(0, len(slots), GROUP):
        left, right = [], []
        for s in range(g, g + GROUP):
            piece, j = slots[s]
            left.append(piece[j])
            right.append(panel[pl.ds(pl.multiple_of(where[s] * BLK, BLK), BLK), :])
        left_high, left_low = split(jnp.concatenate(left, axis=1))
        right_high, right_low = split(jnp.concatenate(right, axis=0))
        dot = lambda a, b: jnp.dot(a, b, preferred_element_type=jnp.float32)
        term = (dot(left_high, right_low) + dot(left_low, right_high)) + dot(left_high, right_high)
        total[...] = term if g == 0 else total[...] + term


def mask_pair(block, live, i):
    return jnp.concatenate(
        [live[CORE * i + c] * block[:, c * BLK : (c + 1) * BLK] for c in range(CORE)], axis=1
    )


def square_body(sizes, where, live, *refs):
    *pieces, panel, keep, give, total = refs
    partial_product(sizes, where, pieces, panel, total)
    core = where[sum(sizes)]
    for q in range(keep.shape[0] // BLK):
        for out, i in ((keep, CORE * q + core), (give, CORE * q + 1 - core)):
            block = total[pl.ds(pl.multiple_of(i * BLK, BLK), BLK), :]
            out[pl.ds(q * BLK, BLK), :] = mask_pair(block, live, i)


def step_body(sizes, where, live, *refs):
    *pieces, panel, kept, given, keep, give, total = refs
    partial_product(sizes, where, pieces, panel, total)
    core = where[sum(sizes)]
    first = core == 0
    for i in range(keep.shape[0] // BLK):
        rows = pl.ds(i * BLK, BLK)
        q = pl.ds(i // CORE * BLK, BLK)
        square = jnp.where(core == i % CORE, kept[q, :], given[q, :])
        part = 3.0 * square - 2.0 * mask_pair(total[rows, :], live, i)
        keep[rows, :] = jnp.where(first, part[:, :BLK], part[:, BLK:])
        give[rows, :] = jnp.where(first, part[:, BLK:], part[:, :BLK])


def call(body, where, live, pieces, panel, extra, shape):
    rows = pieces[0].shape[1]
    sizes = [p.shape[0] for p in pieces]
    slots = sum(sizes)
    width = panel.shape[1]
    vmem = pl.BlockSpec(memory_space=pltpu.VMEM)
    out = jax.ShapeDtypeStruct(shape, jnp.float32)
    return pl.pallas_call(
        lambda *refs: body(sizes, *refs),
        out_shape=(out, out),
        in_specs=[pl.BlockSpec(memory_space=pltpu.SMEM)] * 2 + [vmem] * (len(pieces) + 1 + len(extra)),
        out_specs=(vmem, vmem),
        scratch_shapes=[pltpu.VMEM((rows, width), jnp.float32)],
        compiler_params=pltpu.CompilerParams(vmem_limit_bytes=16 << 20),
        cost_estimate=pl.CostEstimate(
            flops=6 * rows * slots * BLK * width,
            bytes_accessed=4 * (slots * BLK * (rows + width) + 2 * rows * width),
            transcendentals=0,
        ),
    )(where, live, *pieces, panel, *extra)


def local(density, pattern):
    rows_dev, cols_dev = density.shape
    row_number = lax.axis_index("row")
    col_index = lax.axis_index("col")
    core = col_index % CORE
    block_count = cols_dev * lax.axis_size("col") // BLK
    row_blocks = rows_dev // BLK
    listed = jnp.any(
        pattern[:, :, None] == jnp.arange(block_count, dtype=jnp.int32)[None, None, :], axis=1
    ).astype(jnp.float32)
    block_live = jnp.maximum(listed, listed.T)
    my_rows = lax.dynamic_slice_in_dim(block_live, row_number * row_blocks, row_blocks, 0)
    chip = lax.dynamic_slice_in_dim(my_rows, col_index - core, CORE, 1)
    tile_live = jnp.where(core == 0, chip[:, 0], chip[:, 1])
    tile_mask = jnp.repeat(tile_live, BLK)[:, None]
    live = chip.reshape(-1)
    global_rows = row_number * rows_dev + jnp.arange(rows_dev, dtype=jnp.int32)
    global_cols = col_index * cols_dev + jnp.arange(cols_dev, dtype=jnp.int32)
    identity = (global_rows[:, None] == global_cols[None, :]).astype(jnp.float32)
    current = 0.5 * identity + 0.45 / jnp.sqrt(jnp.float32(2 * NNZ * BLK)) * tile_mask * density
    where = piece_columns(col_index)
    for purify_round in range(ITERS):
        panel = lax.all_gather(to_pair(current, core), "row", axis=0, tiled=True)
        pieces = gather_cols(current)
        kept, given = call(
            square_body, where, live, pieces, panel, [], (rows_dev // CORE, CORE * BLK)
        )
        square = kept + send(given, TWIN)
        square_panel = gather_rows(square, "row")
        keep, give = call(
            step_body, where, live, pieces, square_panel, [kept, given], (rows_dev, BLK)
        )
        current = keep + send(give, TWIN)
    return current


def solution(mesh):
    return jax.shard_map(
        local,
        mesh=mesh,
        in_specs=(P("row", "col"), P()),
        out_specs=P("row", "col"),
        check_vma=False,
    )
```

time: 323 us -> 234 us (0.72)
  waiting for transfers between devices: 182 us -> 87.7 us
  starting transfers between devices: 5.99 us -> 46 us
  blocking collectives: 92.2 us -> 62.2 us
  matrix products: 21.7 us -> 0 us
  Pallas kernels: 0 us -> 10.9 us
  local copies, waits for them, and re-layouts: 4.07 us -> 8.4 us
    all_gather x2, waiting for transfers between devices: 154 us -> 0.01 us  [local(): panel = lax.all_gather(to_pair(current, core), 'row', axis=0, tiled=True)]
    ppermute x0 -> x24, waiting for transfers between devices: none -> 87.7 us  [send(): return lax.ppermute(v, 'col', pairs)]
    ppermute x0 -> x24, starting transfers between devices: none -> 46 us  [send(): return lax.ppermute(v, 'col', pairs)]
    all_to_all x3 -> x2, blocking collectives: 92.2 us -> 62.2 us  [gather_rows(): got = lax.all_to_all(copies, name, 0, 0)]
    all_to_all x1 -> x0, waiting for transfers between devices: 28.8 us -> none  [gather_rows(): got = lax.all_to_all(copies, name, 0, 0)]
    dot_general x4 -> x0, matrix products: 21.7 us -> none  [product(): jnp.dot(left, right, precision=lax.Precision.HIGH, preferred_element_type...]
    pallas_call x0 -> x4, Pallas kernels: none -> 10.9 us  [call(): pl.pallas_call(lambda *refs: body(sizes, *refs), out_shape=(out, out), in...]
    unnamed x5 -> x25, local copies, waits for them, and re-layouts: 0.1 us -> 7.65 us
  transfers between devices with their start and end apart: 3 -> 26, of which waited for: 3 -> 18; matrix products, arithmetic and copies ran while one was open for 1% -> 0% of each run, Pallas kernels for 0% -> 0%
where the time goes in v4:
time: 234 us
  waiting for transfers between devices  87.7 us (37%)
  blocking collectives  62.2 us (27%)
  starting transfers between devices  46 us (20%)
  between operations  13.6 us (6%)
  Pallas kernels  10.9 us (5%)
  local copies, waits for them, and re-layouts  8.4 us (4%)
  other arithmetic  4.79 us (2%)
    ppermute x24, waiting for transfers between devices, send(): return lax.ppermute(v, 'col', pairs)  87.7 us
    all_to_all x2, blocking collectives, gather_rows(): got = lax.all_to_all(copies, name, 0, 0)  62.2 us
    ppermute x24, starting transfers between devices, send(): return lax.ppermute(v, 'col', pairs)  46 us
    pallas_call x4, Pallas kernels, call(): pl.pallas_call(lambda *refs: body(sizes, *refs), out_shape=(out, out), in...  10.9 us
    unnamed x25, local copies, waits for them, and re-layouts  7.65 us
  transfers between devices with their start and end apart: 26, of which 18 were waited for; matrix products, arithmetic and copies ran while one was open for 0% of the time, Pallas kernels for 0%

profile of v4, /device:TPU:1, one launch (start us, length us, event | category | flops | bytes accessed | tf_op | source)
XLA Modules:
  0.0 233.7 jit_solution(10467064455775182295)
XLA Ops:
  8.9 3.3 %collective-permute-start.9 = (f32[2,128,128]{2,1,0:T(8,128)S(1)}, f32[2,128,128]{2,1,0:T(8,128)S(1)}, u32[]{:S(2)}, u32[]{:S(2)}) collective-permute-start(f32[2,128,128]{2,1,0:T(8,128)S(1)} %select_bitcast_fusion.1), channel_id=1, source_target_pairs={{0,1},{1,0},{2,3},{3,2},{4,5},{5,4},{6,7},{7,6},{8,9},{9,8},{10,11... | collective-permute-start | bytes 393224 | tf_op jit(solution)/shard_map/ppermute | solution.py:27
  15.4 7.8 %collective-permute-done = f32[512,128]{1,0:T(8,128)S(1)} collective-permute-done((f32[512,128]{1,0:T(8,128)S(1)}, f32[512,128]{1,0:T(8,128)S(1)}, u32[]{:S(2)}, u32[]{:S(2)}) %collective-permute-start) | collective-permute-done | bytes 262176 | tf_op jit(solution)/shard_map/ppermute | solution.py:27
  23.2 3.9 %collective-permute-start.2 = (f32[2,512,128]{2,1,0:T(8,128)S(1)}, f32[2,512,128]{2,1,0:T(8,128)S(1)}, u32[]{:S(2)}, u32[]{:S(2)}) collective-permute-start(f32[2,512,128]{2,1,0:T(8,128)S(1)} %pad_maximum_fusion.refs_2_), channel_id=1, source_target_pairs={{0,14},{1,15},{2,0},{3,1},{4,2},{5,3},{6,4},{7,5},{8,6},{9,7},{10,... | collective-permute-start | bytes 1572872 | tf_op jit(solution)/shard_map/ppermute | solution.py:27
  27.2 10.0 %collective-permute-done.2.refs_4_ = f32[2,512,128]{2,1,0:T(8,128)S(1)} collective-permute-done((f32[2,512,128]{2,1,0:T(8,128)S(1)}, f32[2,512,128]{2,1,0:T(8,128)S(1)}, u32[]{:S(2)}, u32[]{:S(2)}) %collective-permute-start.2) | collective-permute-done | bytes 524320 | tf_op jit(solution)/shard_map/ppermute | solution.py:27
  37.2 3.4 %collective-permute-start.4 = (f32[2,512,128]{2,1,0:T(8,128)S(1)}, f32[2,512,128]{2,1,0:T(8,128)S(1)}, u32[]{:S(2)}, u32[]{:S(2)}) collective-permute-start(f32[2,512,128]{2,1,0:T(8,128)S(1)} %collective-permute-done.2.refs_4_), channel_id=1, source_target_pairs={{0,14},{1,15},{2,0},{3,1},{4,2},{5,3},{6,4},{7,5},{8,6},{9,7},{10,... | collective-permute-start | bytes 1572872 | tf_op jit(solution)/shard_map/ppermute | solution.py:27
  40.6 9.1 %collective-permute-done.4.refs_6_ = f32[2,512,128]{2,1,0:T(8,128)S(1)} collective-permute-done((f32[2,512,128]{2,1,0:T(8,128)S(1)}, f32[2,512,128]{2,1,0:T(8,128)S(1)}, u32[]{:S(2)}, u32[]{:S(2)}) %collective-permute-start.4) | collective-permute-done | bytes 524320 | tf_op jit(solution)/shard_map/ppermute | solution.py:27
  49.7 3.4 %collective-permute-start.6 = (f32[2,512,128]{2,1,0:T(8,128)S(1)}, f32[2,512,128]{2,1,0:T(8,128)S(1)}, u32[]{:S(2)}, u32[]{:S(2)}) collective-permute-start(f32[2,512,128]{2,1,0:T(8,128)S(1)} %collective-permute-done.4.refs_6_), channel_id=1, source_target_pairs={{0,14},{1,15},{2,0},{3,1},{4,2},{5,3},{6,4},{7,5},{8,6},{9,7},{10,... | collective-permute-start | bytes 1572872 | tf_op jit(solution)/shard_map/ppermute | solution.py:27
  53.3 8.0 %collective-permute-done.6.refs_8_ = f32[2,512,128]{2,1,0:T(8,128)S(1)} collective-permute-done((f32[2,512,128]{2,1,0:T(8,128)S(1)}, f32[2,512,128]{2,1,0:T(8,128)S(1)}, u32[]{:S(2)}, u32[]{:S(2)}) %collective-permute-start.6) | collective-permute-done | bytes 524320 | tf_op jit(solution)/shard_map/ppermute | solution.py:27
  61.3 3.5 %collective-permute-start.8 = (f32[1,512,128]{2,1,0:T(8,128)S(1)}, f32[1,512,128]{2,1,0:T(8,128)S(1)}, u32[]{:S(2)}, u32[]{:S(2)}) collective-permute-start(f32[1,512,128]{2,1,0:T(8,128)S(1)} %slice.45), channel_id=1, source_target_pairs={{0,14},{1,15},{2,0},{3,1},{4,2},{5,3},{6,4},{7,5},{8,6},{9,7},{10,... | collective-permute-start | bytes 786440 | tf_op jit(solution)/shard_map/ppermute | solution.py:27
  65.0 3.1 %collective-permute-done.8.refs_10_ = f32[1,512,128]{2,1,0:T(8,128)S(1)} collective-permute-done((f32[1,512,128]{2,1,0:T(8,128)S(1)}, f32[1,512,128]{2,1,0:T(8,128)S(1)}, u32[]{:S(2)}, u32[]{:S(2)}) %collective-permute-start.8) | collective-permute-done | bytes 262176 | tf_op jit(solution)/shard_map/ppermute | solution.py:27
  68.1 3.2 %collective-permute-done.7.refs_9_ = f32[1,512,128]{2,1,0:T(8,128)S(1)} collective-permute-done((f32[1,512,128]{2,1,0:T(8,128)S(1)}, f32[1,512,128]{2,1,0:T(8,128)S(1)}, u32[]{:S(2)}, u32[]{:S(2)}) %collective-permute-start.7) | collective-permute-done | bytes 262176 | tf_op jit(solution)/shard_map/ppermute | solution.py:27
  74.6 3.0 %shard_map.37 = (f32[256,256]{1,0:T(8,128)S(1)}, f32[256,256]{1,0:T(8,128)S(1)}) custom-call(s32[17]{0:T(128)S(1)} %pad_add_fusion.refs_0_, f32[8]{0:T(128)S(1)} %reshape.53.refs_1_, f32[2,512,128]{2,1,0:T(8,128)S(1)} %pad_maximum_fusion.refs_2_, f32[2,512,128]{2,1,0:T(8,128)S(1)} %collective-permute-done.1.refs_3_, ...), custom_call_target="tpu_custom_call" | custom-call | flops 1610612736 | bytes 7340032 | tf_op jit(solution)/shard_map/pallas_call | solution.py:121
  77.6 5.5 %collective-permute-start.10 = (f32[256,256]{1,0:T(8,128)S(1)}, f32[256,256]{1,0:T(8,128)S(1)}, u32[]{:S(2)}, u32[]{:S(2)}) collective-permute-start(f32[256,256]{1,0:T(8,128)S(1)} %get-tuple-element.14.refs_13_), channel_id=1, source_target_pairs={{0,1},{1,0},{2,3},{3,2},{4,5},{5,4},{6,7},{7,6},{8,9},{9,8},{10,11... | collective-permute-start | bytes 786440 | tf_op jit(solution)/shard_map/ppermute | solution.py:27
  84.5 31.2 %all_to_all.10 = f32[8,256,256]{2,1,0:T(8,128)S(1)} all-to-all(f32[8,256,256]{2,1,0:T(8,128)S(1)} %broadcast_in_dim.10), channel_id=1, replica_groups=mesh['row'=8,'col'=32] {'row'}, dimensions={0} | all-to-all | bytes 4194304 | tf_op jit(solution)/shard_map/all_to_all | solution.py:33
  115.7 2.9 %shard_map.38 = (f32[512,128]{1,0:T(8,128)S(1)}, f32[512,128]{1,0:T(8,128)S(1)}) custom-call(s32[17]{0:T(128)S(1)} %pad_add_fusion.refs_0_, f32[8]{0:T(128)S(1)} %reshape.53.refs_1_, f32[2,512,128]{2,1,0:T(8,128)S(1)} %pad_maximum_fusion.refs_2_, f32[2,512,128]{2,1,0:T(8,128)S(1)} %collective-permute-done.1.refs_3_, ...), custom_call_target="tpu_custom_call" | custom-call | flops 1610612736 | bytes 7340032 | tf_op jit(solution)/shard_map/pallas_call | solution.py:121
  124.2 2.5 %collective-permute-start.12 = (f32[512,128]{1,0:T(8,128)S(1)}, f32[512,128]{1,0:T(8,128)S(1)}, u32[]{:S(2)}, u32[]{:S(2)}) collective-permute-start(f32[512,128]{1,0:T(8,128)S(1)} %add.104), channel_id=1, source_target_pairs={{0,16},{1,17},{2,18},{3,19},{4,20},{5,21},{6,22},{7,23},{8,24},{9,... | collective-permute-start | bytes 786440 | tf_op jit(solution)/shard_map/ppermute | solution.py:27
  126.7 6.6 %collective-permute-done.12 = f32[512,128]{1,0:T(8,128)S(1)} collective-permute-done((f32[512,128]{1,0:T(8,128)S(1)}, f32[512,128]{1,0:T(8,128)S(1)}, u32[]{:S(2)}, u32[]{:S(2)}) %collective-permute-start.12) | collective-permute-done | bytes 262176 | tf_op jit(solution)/shard_map/ppermute | solution.py:27
  134.9 9.3 %collective-permute-done.14.refs_4_ = f32[2,512,128]{2,1,0:T(8,128)S(1)} collective-permute-done((f32[2,512,128]{2,1,0:T(8,128)S(1)}, f32[2,512,128]{2,1,0:T(8,128)S(1)}, u32[]{:S(2)}, u32[]{:S(2)}) %collective-permute-start.14) | collective-permute-done | bytes 524320 | tf_op jit(solution)/shard_map/ppermute | solution.py:27
  145.7 9.0 %collective-permute-done.16.refs_6_ = f32[2,512,128]{2,1,0:T(8,128)S(1)} collective-permute-done((f32[2,512,128]{2,1,0:T(8,128)S(1)}, f32[2,512,128]{2,1,0:T(8,128)S(1)}, u32[]{:S(2)}, u32[]{:S(2)}) %collective-permute-start.16) | collective-permute-done | bytes 524320 | tf_op jit(solution)/shard_map/ppermute | solution.py:27
  157.2 8.0 %collective-permute-done.18.refs_8_ = f32[2,512,128]{2,1,0:T(8,128)S(1)} collective-permute-done((f32[2,512,128]{2,1,0:T(8,128)S(1)}, f32[2,512,128]{2,1,0:T(8,128)S(1)}, u32[]{:S(2)}, u32[]{:S(2)}) %collective-permute-start.18) | collective-permute-done | bytes 524320 | tf_op jit(solution)/shard_map/ppermute | solution.py:27
  165.2 2.6 %collective-permute-start.20 = (f32[1,512,128]{2,1,0:T(8,128)S(1)}, f32[1,512,128]{2,1,0:T(8,128)S(1)}, u32[]{:S(2)}, u32[]{:S(2)}) collective-permute-start(f32[1,512,128]{2,1,0:T(8,128)S(1)} %slice.49), channel_id=1, source_target_pairs={{0,14},{1,15},{2,0},{3,1},{4,2},{5,3},{6,4},{7,5},{8,6},{9,7},{10,... | collective-permute-start | bytes 786440 | tf_op jit(solution)/shard_map/ppermute | solution.py:27
  167.9 4.8 %collective-permute-done.20.refs_10_ = f32[1,512,128]{2,1,0:T(8,128)S(1)} collective-permute-done((f32[1,512,128]{2,1,0:T(8,128)S(1)}, f32[1,512,128]{2,1,0:T(8,128)S(1)}, u32[]{:S(2)}, u32[]{:S(2)}) %collective-permute-start.20) | collective-permute-done | bytes 262176 | tf_op jit(solution)/shard_map/ppermute | solution.py:27
  181.6 6.6 %collective-permute-start.22 = (f32[256,256]{1,0:T(8,128)S(1)}, f32[256,256]{1,0:T(8,128)S(1)}, u32[]{:S(2)}, u32[]{:S(2)}) collective-permute-start(f32[256,256]{1,0:T(8,128)S(1)} %get-tuple-element.18.refs_13_), channel_id=1, source_target_pairs={{0,1},{1,0},{2,3},{3,2},{4,5},{5,4},{6,7},{7,6},{8,9},{9,8},{10,11... | collective-permute-start | bytes 786440 | tf_op jit(solution)/shard_map/ppermute | solution.py:27
  189.6 31.0 %all_to_all.11 = f32[8,256,256]{2,1,0:T(8,128)S(1)} all-to-all(f32[8,256,256]{2,1,0:T(8,128)S(1)} %broadcast_in_dim.11), channel_id=1, replica_groups=mesh['row'=8,'col'=32] {'row'}, dimensions={0} | all-to-all | bytes 4194304 | tf_op jit(solution)/shard_map/all_to_all | solution.py:33
  (93 shorter events, 38.2 us)
Async XLA Ops:
  6.5 65.5 %all-gather.3.cloned.1.call-start = ((), (), s32[]{:S(2)}) async-start(), calls=%async_computation.2 | async-start | bytes 2359296 | tf_op jit(solution)/shard_map/all_gather | solution.py:158
  8.9 4.3 %collective-permute-start.9 = (f32[2,128,128]{2,1,0:T(8,128)S(1)}, f32[2,128,128]{2,1,0:T(8,128)S(1)}, u32[]{:S(2)}, u32[]{:S(2)}) collective-permute-start(f32[2,128,128]{2,1,0:T(8,128)S(1)} %select_bitcast_fusion.1), channel_id=1, source_target_pairs={{0,1},{1,0},{2,3},{3,2},{4,5},{5,4},{6,7},{7,6},{8,9},{9,8},{10,11... | collective-permute-start | bytes 393224 | tf_op jit(solution)/shard_map/ppermute | solution.py:27
  14.0 161.5 %all-gather.5.cloned.1.call-start = ((), (), s32[]{:S(2)}) async-start(), calls=%async_computation.3 | async-start | bytes 2359296 | tf_op jit(solution)/shard_map/all_gather | solution.py:158
  14.1 9.1 %collective-permute-start = (f32[512,128]{1,0:T(8,128)S(1)}, f32[512,128]{1,0:T(8,128)S(1)}, u32[]{:S(2)}, u32[]{:S(2)}) collective-permute-start(f32[512,128]{1,0:T(8,128)S(1)} %multiply_add_fusion), channel_id=1, source_target_pairs={{0,16},{1,17},{2,18},{3,19},{4,20},{5,21},{6,22},{7,23},{8,24},{9,... | collective-permute-start | bytes 786440 | tf_op jit(solution)/shard_map/ppermute | solution.py:27
  23.2 13.9 %collective-permute-start.2 = (f32[2,512,128]{2,1,0:T(8,128)S(1)}, f32[2,512,128]{2,1,0:T(8,128)S(1)}, u32[]{:S(2)}, u32[]{:S(2)}) collective-permute-start(f32[2,512,128]{2,1,0:T(8,128)S(1)} %pad_maximum_fusion.refs_2_), channel_id=1, source_target_pairs={{0,14},{1,15},{2,0},{3,1},{4,2},{5,3},{6,4},{7,5},{8,6},{9,7},{10,... | collective-permute-start | bytes 1572872 | tf_op jit(solution)/shard_map/ppermute | solution.py:27
  27.1 13.4 %collective-permute-start.1 = (f32[2,512,128]{2,1,0:T(8,128)S(1)}, f32[2,512,128]{2,1,0:T(8,128)S(1)}, u32[]{:S(2)}, u32[]{:S(2)}) collective-permute-start(f32[2,512,128]{2,1,0:T(8,128)S(1)} %pad_maximum_fusion.refs_2_), channel_id=1, source_target_pairs={{0,2},{1,3},{2,4},{3,5},{4,6},{5,7},{6,8},{7,9},{8,10},{9,11},{10,... | collective-permute-start | bytes 1572872 | tf_op jit(solution)/shard_map/ppermute | solution.py:27
  37.2 12.5 %collective-permute-start.4 = (f32[2,512,128]{2,1,0:T(8,128)S(1)}, f32[2,512,128]{2,1,0:T(8,128)S(1)}, u32[]{:S(2)}, u32[]{:S(2)}) collective-permute-start(f32[2,512,128]{2,1,0:T(8,128)S(1)} %collective-permute-done.2.refs_4_), channel_id=1, source_target_pairs={{0,14},{1,15},{2,0},{3,1},{4,2},{5,3},{6,4},{7,5},{8,6},{9,7},{10,... | collective-permute-start | bytes 1572872 | tf_op jit(solution)/shard_map/ppermute | solution.py:27
  40.6 12.5 %collective-permute-start.3 = (f32[2,512,128]{2,1,0:T(8,128)S(1)}, f32[2,512,128]{2,1,0:T(8,128)}, u32[]{:S(2)}, u32[]{:S(2)}) collective-permute-start(f32[2,512,128]{2,1,0:T(8,128)S(1)} %collective-permute-done.1.refs_3_), channel_id=1, source_target_pairs={{0,2},{1,3},{2,4},{3,5},{4,6},{5,7},{6,8},{7,9},{8,10},{9,11},{10,... | collective-permute-start | bytes 1572872 | tf_op jit(solution)/shard_map/ppermute | solution.py:27
  49.7 11.6 %collective-permute-start.6 = (f32[2,512,128]{2,1,0:T(8,128)S(1)}, f32[2,512,128]{2,1,0:T(8,128)S(1)}, u32[]{:S(2)}, u32[]{:S(2)}) collective-permute-start(f32[2,512,128]{2,1,0:T(8,128)S(1)} %collective-permute-done.4.refs_6_), channel_id=1, source_target_pairs={{0,14},{1,15},{2,0},{3,1},{4,2},{5,3},{6,4},{7,5},{8,6},{9,7},{10,... | collective-permute-start | bytes 1572872 | tf_op jit(solution)/shard_map/ppermute | solution.py:27
  53.1 11.7 %collective-permute-start.5 = (f32[2,512,128]{2,1,0:T(8,128)}, f32[2,512,128]{2,1,0:T(8,128)S(1)}, u32[]{:S(2)}, u32[]{:S(2)}) collective-permute-start(f32[2,512,128]{2,1,0:T(8,128)} %collective-permute-done.3.refs_5_), channel_id=1, source_target_pairs={{0,2},{1,3},{2,4},{3,5},{4,6},{5,7},{6,8},{7,9},{8,10},{9,11},{10,... | collective-permute-start | bytes 1572872 | tf_op jit(solution)/shard_map/ppermute | solution.py:27
  61.3 6.8 %collective-permute-start.8 = (f32[1,512,128]{2,1,0:T(8,128)S(1)}, f32[1,512,128]{2,1,0:T(8,128)S(1)}, u32[]{:S(2)}, u32[]{:S(2)}) collective-permute-start(f32[1,512,128]{2,1,0:T(8,128)S(1)} %slice.45), channel_id=1, source_target_pairs={{0,14},{1,15},{2,0},{3,1},{4,2},{5,3},{6,4},{7,5},{8,6},{9,7},{10,... | collective-permute-start | bytes 786440 | tf_op jit(solution)/shard_map/ppermute | solution.py:27
  64.8 6.5 %collective-permute-start.7 = (f32[1,512,128]{2,1,0:T(8,128)S(1)}, f32[1,512,128]{2,1,0:T(8,128)S(1)}, u32[]{:S(2)}, u32[]{:S(2)}) collective-permute-start(f32[1,512,128]{2,1,0:T(8,128)S(1)} %slice.44), channel_id=1, source_target_pairs={{0,2},{1,3},{2,4},{3,5},{4,6},{5,7},{6,8},{7,9},{8,10},{9,11},{10,... | collective-permute-start | bytes 786440 | tf_op jit(solution)/shard_map/ppermute | solution.py:27
  77.6 6.6 %collective-permute-start.10 = (f32[256,256]{1,0:T(8,128)S(1)}, f32[256,256]{1,0:T(8,128)S(1)}, u32[]{:S(2)}, u32[]{:S(2)}) collective-permute-start(f32[256,256]{1,0:T(8,128)S(1)} %get-tuple-element.14.refs_13_), channel_id=1, source_target_pairs={{0,1},{1,0},{2,3},{3,2},{4,5},{5,4},{6,7},{7,6},{8,9},{9,8},{10,11... | collective-permute-start | bytes 786440 | tf_op jit(solution)/shard_map/ppermute | solution.py:27
  118.7 3.3 %collective-permute-start.11 = (f32[512,128]{1,0:T(8,128)S(1)}, f32[512,128]{1,0:T(8,128)S(1)}, u32[]{:S(2)}, u32[]{:S(2)}) collective-permute-start(f32[512,128]{1,0:T(8,128)S(1)} %get-tuple-element.16), channel_id=1, source_target_pairs={{0,1},{1,0},{2,3},{3,2},{4,5},{5,4},{6,7},{7,6},{8,9},{9,8},{10,11... | collective-permute-start | bytes 786440 | tf_op jit(solution)/shard_map/ppermute | solution.py:27
  124.2 9.1 %collective-permute-start.12 = (f32[512,128]{1,0:T(8,128)S(1)}, f32[512,128]{1,0:T(8,128)S(1)}, u32[]{:S(2)}, u32[]{:S(2)}) collective-permute-start(f32[512,128]{1,0:T(8,128)S(1)} %add.104), channel_id=1, source_target_pairs={{0,16},{1,17},{2,18},{3,19},{4,20},{5,21},{6,22},{7,23},{8,24},{9,... | collective-permute-start | bytes 786440 | tf_op jit(solution)/shard_map/ppermute | solution.py:27
  133.4 10.9 %collective-permute-start.14 = (f32[2,512,128]{2,1,0:T(8,128)S(1)}, f32[2,512,128]{2,1,0:T(8,128)S(1)}, u32[]{:S(2)}, u32[]{:S(2)}) collective-permute-start(f32[2,512,128]{2,1,0:T(8,128)S(1)} %pad_maximum_fusion.1.refs_2_), channel_id=1, source_target_pairs={{0,14},{1,15},{2,0},{3,1},{4,2},{5,3},{6,4},{7,5},{8,6},{9,7},{10,... | collective-permute-start | bytes 1572872 | tf_op jit(solution)/shard_map/ppermute | solution.py:27
  133.4 12.3 %collective-permute-start.13 = (f32[2,512,128]{2,1,0:T(8,128)S(1)}, f32[2,512,128]{2,1,0:T(8,128)S(1)}, u32[]{:S(2)}, u32[]{:S(2)}) collective-permute-start(f32[2,512,128]{2,1,0:T(8,128)S(1)} %pad_maximum_fusion.1.refs_2_), channel_id=1, source_target_pairs={{0,2},{1,3},{2,4},{3,5},{4,6},{5,7},{6,8},{7,9},{8,10},{9,11},{10,... | collective-permute-start | bytes 1572872 | tf_op jit(solution)/shard_map/ppermute | solution.py:27
  144.2 10.5 %collective-permute-start.16 = (f32[2,512,128]{2,1,0:T(8,128)S(1)}, f32[2,512,128]{2,1,0:T(8,128)S(1)}, u32[]{:S(2)}, u32[]{:S(2)}) collective-permute-start(f32[2,512,128]{2,1,0:T(8,128)S(1)} %collective-permute-done.14.refs_4_), channel_id=1, source_target_pairs={{0,14},{1,15},{2,0},{3,1},{4,2},{5,3},{6,4},{7,5},{8,6},{9,7},{10,... | collective-permute-start | bytes 1572872 | tf_op jit(solution)/shard_map/ppermute | solution.py:27
  145.7 11.5 %collective-permute-start.15 = (f32[2,512,128]{2,1,0:T(8,128)S(1)}, f32[2,512,128]{2,1,0:T(8,128)S(1)}, u32[]{:S(2)}, u32[]{:S(2)}) collective-permute-start(f32[2,512,128]{2,1,0:T(8,128)S(1)} %collective-permute-done.13.refs_3_), channel_id=1, source_target_pairs={{0,2},{1,3},{2,4},{3,5},{4,6},{5,7},{6,8},{7,9},{8,10},{9,11},{10,... | collective-permute-start | bytes 1572872 | tf_op jit(solution)/shard_map/ppermute | solution.py:27
  154.7 10.5 %collective-permute-start.18 = (f32[2,512,128]{2,1,0:T(8,128)S(1)}, f32[2,512,128]{2,1,0:T(8,128)S(1)}, u32[]{:S(2)}, u32[]{:S(2)}) collective-permute-start(f32[2,512,128]{2,1,0:T(8,128)S(1)} %collective-permute-done.16.refs_6_), channel_id=1, source_target_pairs={{0,14},{1,15},{2,0},{3,1},{4,2},{5,3},{6,4},{7,5},{8,6},{9,7},{10,... | collective-permute-start | bytes 1572872 | tf_op jit(solution)/shard_map/ppermute | solution.py:27
  157.2 10.6 %collective-permute-start.17 = (f32[2,512,128]{2,1,0:T(8,128)S(1)}, f32[2,512,128]{2,1,0:T(8,128)S(1)}, u32[]{:S(2)}, u32[]{:S(2)}) collective-permute-start(f32[2,512,128]{2,1,0:T(8,128)S(1)} %collective-permute-done.15.refs_5_), channel_id=1, source_target_pairs={{0,2},{1,3},{2,4},{3,5},{4,6},{5,7},{6,8},{7,9},{8,10},{9,11},{10,... | collective-permute-start | bytes 1572872 | tf_op jit(solution)/shard_map/ppermute | solution.py:27
  165.2 7.5 %collective-permute-start.20 = (f32[1,512,128]{2,1,0:T(8,128)S(1)}, f32[1,512,128]{2,1,0:T(8,128)S(1)}, u32[]{:S(2)}, u32[]{:S(2)}) collective-permute-start(f32[1,512,128]{2,1,0:T(8,128)S(1)} %slice.49), channel_id=1, source_target_pairs={{0,14},{1,15},{2,0},{3,1},{4,2},{5,3},{6,4},{7,5},{8,6},{9,7},{10,... | collective-permute-start | bytes 786440 | tf_op jit(solution)/shard_map/ppermute | solution.py:27
  167.9 7.0 %collective-permute-start.19 = (f32[1,512,128]{2,1,0:T(8,128)S(1)}, f32[1,512,128]{2,1,0:T(8,128)S(1)}, u32[]{:S(2)}, u32[]{:S(2)}) collective-permute-start(f32[1,512,128]{2,1,0:T(8,128)S(1)} %slice.48), channel_id=1, source_target_pairs={{0,2},{1,3},{2,4},{3,5},{4,6},{5,7},{6,8},{7,9},{8,10},{9,11},{10,... | collective-permute-start | bytes 786440 | tf_op jit(solution)/shard_map/ppermute | solution.py:27
  181.6 7.7 %collective-permute-start.22 = (f32[256,256]{1,0:T(8,128)S(1)}, f32[256,256]{1,0:T(8,128)S(1)}, u32[]{:S(2)}, u32[]{:S(2)}) collective-permute-start(f32[256,256]{1,0:T(8,128)S(1)} %get-tuple-element.18.refs_13_), channel_id=1, source_target_pairs={{0,1},{1,0},{2,3},{3,2},{4,5},{5,4},{6,7},{7,6},{8,9},{9,8},{10,11... | collective-permute-start | bytes 786440 | tf_op jit(solution)/shard_map/ppermute | solution.py:27
  (14 other events, 149.6 us)
Sparse Core Ops, SparseCore 0:
  14.1 55.3 all-gather.2
  124.3 49.5 all-gather.4
